TPU v7x, 32 devices: a whole 2x2x4 slice. The times are simulated.
32 devices in a mesh: cfg: 1, node: 32 (over z, y, x, core), pair: 1.
Axes of the slice: x: 2, y: 2, z: 4, core: 2. Of those that a mesh axis runs over, the one named last changes fastest.
Arguments:
- node_blocks: float32 [256, 2, 256, 256], P(('cfg', 'node'), None, None, 'pair'), may hold values from -1.5 to 1.5
- node_slot: int32 [256], replicated, may hold values from 0 to 255, as said below
- pair_list: int32 [128, 2], replicated, may hold values from 0 to 255, as said below
- second_list: int32 [128, 2], replicated, may hold values from 0 to 127, as said below
- targets: int32 [128], replicated, may hold values from 0 to 63, as said below
- spin_signs: int32 [128], replicated, may hold values from -1 to 1, as said below
Outputs:
- results: float32 [64, 2, 256, 256], P(('cfg', 'node'), None, None, 'pair')
Inputs may be any that keep to these rules, and one draw needn't show every extreme that they name: `node_slot`: A permutation of the slots. `pair_list`: rows b * 4 to (b + 1) * 4 - 1 form block b. The first node of a pair in block b sits at a slot of b * 8 to (b + 1) * 8 - 1. For every block b and every owner o, at most 1 pair of block b has its second node at slots o * 8 to (o + 1) * 8 - 1; one owner supplies exactly 1 such node to every block. `second_list`: rows b * 4 to (b + 1) * 4 - 1 form block b. The first pair of a product in block b lies in block b of the pairs. For every block b and owner o, at most 1 product of block b has its second pair in block o of the pairs; one owner supplies exactly 1 such pair product to every block. `targets`: products of block b target results b * 2 to (b + 1) * 2 - 1. `spin_signs`: each entry is -1 or 1.
All inputs are finite; a program needn't handle non-finite values.
Results may differ from a plain program's by a relative error of at most 0.000098.
Values sent between devices are 32-bit elements; how exact they have to be, the bound alone decides.
No kernel may reach another device: no remote copies, remote signals or barrier semaphores. Data moves between devices by JAX's collectives and lax.ppermute only.
A program may use at most 128 MiB of HBM per device.

v0:
```python
import jax
import jax.numpy as jnp
from jax import lax
from jax.sharding import PartitionSpec as P

NODE_COL = 8
PAIR_COL = 4
RES_COL = 2


def complex_product(left_side, right_side):
    half_width = right_side.shape[3]
    stacked_left = jnp.concatenate([left_side[:, 0], left_side[:, 1]], axis=2)
    real_right = jnp.concatenate([right_side[:, 0], -right_side[:, 1]], axis=1)
    imag_right = jnp.concatenate([right_side[:, 1], right_side[:, 0]], axis=1)
    stacked_right = jnp.concatenate([real_right, imag_right], axis=2)
    joined = jnp.einsum(
        "jmk,jkn->jmn",
        stacked_left,
        stacked_right,
        precision=lax.Precision.HIGHEST,
        preferred_element_type=jnp.float32,
    )
    return jnp.stack([joined[:, :, :half_width], joined[:, :, half_width:]], axis=1)


def send_table(owner_of, local_of, owner_now, capacity):
    matches = (owner_of == owner_now).astype(jnp.int32)
    ranking = jnp.cumsum(matches, axis=1) - 1
    levels = jnp.arange(capacity, dtype=jnp.int32)
    chosen = matches[:, None, :] * (ranking[:, None, :] == levels[None, :, None]).astype(jnp.int32)
    slot_index = jnp.sum(chosen * local_of[:, None, :], axis=2)
    present = jnp.sum(chosen, axis=2)
    return (slot_index.reshape(-1), present.reshape(-1))


def pack_items(local_items, owner_of, local_of, owner_now, capacity):
    slot_index, present = send_table(owner_of, local_of, owner_now, capacity)
    picked = jnp.take(local_items, slot_index, axis=0)
    return picked * present.astype(local_items.dtype)[:, None, None, None]


def receive_index(own_owner, capacity):
    item_count = own_owner.shape[0]
    earlier = jnp.arange(item_count)[:, None] > jnp.arange(item_count)[None, :]
    same_owner = own_owner[:, None] == own_owner[None, :]
    ranking = jnp.sum((earlier & same_owner).astype(jnp.int32), axis=1)
    return own_owner * capacity + ranking


def per_device(node_blocks, node_slot, pair_list, second_list, targets, spin_signs):
    columns = lax.axis_size("node")
    column = lax.axis_index("node")
    capacity = -(-PAIR_COL // columns)
    block_start = column * PAIR_COL
    own_pairs = lax.dynamic_slice_in_dim(pair_list, block_start, PAIR_COL, 0)
    first_slot = node_slot[own_pairs[:, 0]] - column * NODE_COL
    second_slot = node_slot[own_pairs[:, 1]]
    whole_nodes = lax.all_gather(node_blocks, "pair", axis=3, tiled=True)
    first_nodes = jnp.take(whole_nodes, first_slot, axis=0)
    every_slot = node_slot[pair_list[:, 1]].reshape(columns, PAIR_COL)
    outgoing = pack_items(
        node_blocks, every_slot // NODE_COL, every_slot % NODE_COL, column, capacity
    )
    incoming = lax.all_to_all(outgoing, "node", split_axis=0, concat_axis=0, tiled=True)
    second_nodes = jnp.take(incoming, receive_index(second_slot // NODE_COL, capacity), axis=0)
    products = complex_product(first_nodes, second_nodes)
    whole_products = lax.all_gather(products, "pair", axis=3, tiled=True)
    own_seconds = lax.dynamic_slice_in_dim(second_list, block_start, PAIR_COL, 0)
    left_side = jnp.take(whole_products, own_seconds[:, 0] - block_start, axis=0)
    every_right = second_list[:, 1].reshape(columns, PAIR_COL)
    outgoing_products = pack_items(
        products, every_right // PAIR_COL, every_right % PAIR_COL, column, capacity
    )
    incoming_products = lax.all_to_all(
        outgoing_products, "node", split_axis=0, concat_axis=0, tiled=True
    )
    right_side = jnp.take(
        incoming_products, receive_index(own_seconds[:, 1] // PAIR_COL, capacity), axis=0
    )
    own_signs = lax.dynamic_slice_in_dim(spin_signs, block_start, PAIR_COL, 0).astype(jnp.float32)
    seconds = complex_product(left_side, right_side) * own_signs[:, None, None, None]
    own_targets = lax.dynamic_slice_in_dim(targets, block_start, PAIR_COL, 0) - column * RES_COL
    selector = (own_targets[None, :] == jnp.arange(RES_COL)[:, None]).astype(jnp.float32)
    return jnp.einsum(
        "rj,jxmn->rxmn",
        selector,
        seconds,
        precision=lax.Precision.HIGHEST,
        preferred_element_type=jnp.float32,
    )


def solution(mesh):
    placed = (P(("cfg", "node"), None, None, "pair"), P(), P(), P(), P(), P())
    return jax.shard_map(
        per_device,
        mesh=mesh,
        in_specs=placed,
        out_specs=P(("cfg", "node"), None, None, "pair"),
        check_vma=False,
    )
```

profile of v0, /device:TPU:0, one launch (start us, length us, event | category | flops | bytes accessed | tf_op | source)
XLA Modules:
  0.0 830.5 jit_solution(6682804246031589908)
XLA Ops:
  0.0 0.7 slice_reduce_fusion
  1.1 0.7 fusion.47
  1.8 1.3 gather_fusion.2
  3.6 10.1 %gather_fusion.3 = f32[32,2,256,256]{3,2,1,0:T(8,128)} fusion(f32[8,2,256,256]{3,2,1,0:T(8,128)} %param.8, s32[1024]{0:T(1024)S(1)} %pad_clamp_fusion.4), kind=kCustom, calls=%fused_computation.5 | custom fusion | bytes 33554560 | tf_op jit(solution)/shard_map/jit(_take)/gather | solution.py:39
  13.7 11.7 %select_multiply_fusion.1 = f32[32,2,256,256]{3,2,1,0:T(8,128)} fusion(f32[32,2,256,256]{3,2,1,0:T(8,128)} %gather_fusion.3, f32[32]{0:T(128)S(1)} %convert_element_type.47, pred[32]{0:T(512)(128)(4,1)S(1)} %get-tuple-element.33), kind=kLoop, calls=%fused_computation.10 | loop fusion | flops 8388608 | bytes 33554592 | tf_op jit(solution)/shard_map/mul | solution.py:40
  25.4 7.3 all-to-all-start
  32.8 0.6 gather_fusion.4
  33.5 0.6 gather_fusion
  34.2 2.9 gather_fusion.1
  37.1 0.2 convert_reduce_fusion.1
  37.4 0.2 copy_select_fusion.2
  37.6 1.1 slice_bitcast_fusion.11
  38.7 366.6 %all-to-all-done = f32[32,2,256,256]{3,2,1,0:T(8,128)} async-done(((f32[32,2,256,256]{3,2,1,0:T(8,128)}), f32[32,2,256,256]{3,2,1,0:T(8,128)}, u32[]{:S(2)}, u32[]{:S(2)}) %all-to-all-start) | async-done | bytes 16777248 | tf_op jit(solution)/shard_map/all_to_all | solution.py:65
  405.3 6.4 gather_fusion.7
  411.8 0.2 copy_select_fusion.1
  412.3 1.1 copy-done.2
  413.4 3.7 fusion
  417.5 7.8 gather_fusion.6
  425.2 11.7 %select_multiply_fusion = f32[32,2,256,256]{3,2,1,0:T(8,128)} fusion(f32[32,2,256,256]{3,2,1,0:T(8,128)} %gather_fusion.6, f32[32]{0:T(128)S(1)} %convert_element_type.50, pred[32]{0:T(512)(128)(4,1)S(1)} %get-tuple-element.32), kind=kLoop, calls=%fused_computation.9 | loop fusion | flops 8388608 | bytes 33554592 | tf_op jit(solution)/shard_map/mul | solution.py:40
  436.9 4.2 all-to-all-start.1
  441.5 1.5 copy.19
  443.0 2.3 gather_fusion.5
  445.3 0.2 copy_select_fusion
  445.5 1.1 slice_bitcast_fusion.5
  446.6 367.2 %all-to-all-done.1 = f32[32,2,256,256]{3,2,1,0:T(8,128)} async-done(((f32[32,2,256,256]{3,2,1,0:T(8,128)}), f32[32,2,256,256]{3,2,1,0:T(8,128)}, u32[]{:S(2)}, u32[]{:S(2)}) %all-to-all-start.1) | async-done | bytes 16777248 | tf_op jit(solution)/shard_map/all_to_all | solution.py:75
  813.9 6.4 gather_fusion.8
  820.3 0.2 broadcast_select_fusion
  820.8 1.1 copy-done.3
  822.0 3.7 fusion.8
  825.9 0.2 maximum_multiply_fusion
  826.1 3.2 fusion.22
  829.4 1.1 copy.23
  (53 shorter events, 2.3 us)
Async XLA Ops:
  0.0 1.8 copy-start
  25.4 7.3 copy-start.4
  25.4 8.7 %copy-start.5 = (s32[128,2]{0,1:T(2,128)S(1)}, s32[128,2]{0,1:T(2,128)}, u32[]{:S(2)}) copy-start(s32[128,2]{0,1:T(2,128)} %param.11) | copy-start | bytes 3076
  25.4 379.9 %all-to-all-start = ((f32[32,2,256,256]{3,2,1,0:T(8,128)}), f32[32,2,256,256]{3,2,1,0:T(8,128)}, u32[]{:S(2)}, u32[]{:S(2)}) async-start(f32[32,2,256,256]{3,2,1,0:T(8,128)} %select_multiply_fusion.1), calls=%async_computation | async-start | bytes 33554432 | tf_op jit(solution)/shard_map/all_to_all | solution.py:65
  412.2 1.2 copy-start.2
  436.9 4.2 copy-start.6
  436.9 4.2 copy-start.7
  436.9 377.0 %all-to-all-start.1 = ((f32[32,2,256,256]{3,2,1,0:T(8,128)}), f32[32,2,256,256]{3,2,1,0:T(8,128)}, u32[]{:S(2)}, u32[]{:S(2)}) async-start(f32[32,2,256,256]{3,2,1,0:T(8,128)} %select_multiply_fusion), calls=%async_computation.1 | async-start | bytes 33554432 | tf_op jit(solution)/shard_map/all_to_all | solution.py:75
  820.7 1.2 copy-start.3
  826.1 4.3 copy-start.1
where the time goes:
time: 831 us; the launch traced here: 830 us
  waiting for transfers between devices  734 us (88%)
  local copies, waits for them, and re-layouts  47.3 us (6%)
  other arithmetic  26.8 us (3%)
  starting transfers between devices  11.5 us (1%)
  matrix products  10.7 us (1%)
    all_to_all x1, waiting for transfers between devices, per_device(): lax.all_to_all(outgoing_products, 'node', split_axis=0, concat_axis=0, ti...  367 us
    all_to_all x1, waiting for transfers between devices, per_device(): lax.all_to_all(outgoing, 'node', split_axis=0, concat_axis=0, tiled=True)  367 us
    mul x2, other arithmetic, pack_items(): return picked * present.astype(local_items.dtype)[:, None, None, None]  23.4 us
    gather x2, local copies, waits for them, and re-layouts, pack_items(): picked = jnp.take(local_items, slot_index, axis=0)  17.9 us
  transfers between devices with their start and end apart: 2, of which 2 were waited for; matrix products, arithmetic and copies ran while one was open for 1% of the time, Pallas kernels for 0%

commit v1 on v0

v1 whole, which is shorter than its diff:
```python
import jax
import jax.numpy as jnp
from jax import lax
from jax.sharding import PartitionSpec as P

RES_COL = 2


def complex_product(left_side, right_side):
    half_width = right_side.shape[3]
    stacked_left = jnp.concatenate([left_side[:, 0], left_side[:, 1]], axis=2)
    real_right = jnp.concatenate([right_side[:, 0], -right_side[:, 1]], axis=1)
    imag_right = jnp.concatenate([right_side[:, 1], right_side[:, 0]], axis=1)
    stacked_right = jnp.concatenate([real_right, imag_right], axis=2)
    joined = jnp.einsum(
        "jmk,jkn->jmn",
        stacked_left,
        stacked_right,
        precision=lax.Precision.HIGHEST,
        preferred_element_type=jnp.float32,
    )
    return jnp.stack([joined[:, :, :half_width], joined[:, :, half_width:]], axis=1)


def fetch_items(local_items, wanted):
    spread = lax.all_to_all(local_items, "node", split_axis=2, concat_axis=0, tiled=True)
    picked = jnp.take(spread, wanted, axis=0)
    return lax.all_to_all(picked, "node", split_axis=0, concat_axis=2, tiled=True)


def per_device(node_blocks, node_slot, pair_list, second_list, targets, spin_signs):
    columns = lax.axis_size("node")
    column = lax.axis_index("node")
    node_col = node_blocks.shape[0]
    pair_col = pair_list.shape[0] // columns
    block_start = column * pair_col
    second_nodes = fetch_items(node_blocks, node_slot[pair_list[:, 1]])
    own_pairs = lax.dynamic_slice_in_dim(pair_list, block_start, pair_col, 0)
    first_slot = node_slot[own_pairs[:, 0]] - column * node_col
    whole_nodes = lax.all_gather(node_blocks, "pair", axis=3, tiled=True)
    first_nodes = jnp.take(whole_nodes, first_slot, axis=0)
    products = complex_product(first_nodes, second_nodes)
    right_side = fetch_items(products, second_list[:, 1])
    whole_products = lax.all_gather(products, "pair", axis=3, tiled=True)
    own_seconds = lax.dynamic_slice_in_dim(second_list, block_start, pair_col, 0)
    left_side = jnp.take(whole_products, own_seconds[:, 0] - block_start, axis=0)
    own_signs = lax.dynamic_slice_in_dim(spin_signs, block_start, pair_col, 0).astype(jnp.float32)
    seconds = complex_product(left_side, right_side) * own_signs[:, None, None, None]
    own_targets = lax.dynamic_slice_in_dim(targets, block_start, pair_col, 0) - column * RES_COL
    selector = (own_targets[None, :] == jnp.arange(RES_COL)[:, None]).astype(jnp.float32)
    return jnp.einsum(
        "rj,jxmn->rxmn",
        selector,
        seconds,
        precision=lax.Precision.HIGHEST,
        preferred_element_type=jnp.float32,
    )


def solution(mesh):
    placed = (P(("cfg", "node"), None, None, "pair"), P(), P(), P(), P(), P())
    return jax.shard_map(
        per_device,
        mesh=mesh,
        in_specs=placed,
        out_specs=P(("cfg", "node"), None, None, "pair"),
        check_vma=False,
    )
```

time: 831 us -> 309 us (0.37)
  waiting for transfers between devices: 734 us -> 226 us
  other arithmetic: 26.8 us -> 7.45 us
  starting transfers between devices: 11.5 us -> 20.3 us
    all_to_all x2 -> x4, waiting for transfers between devices: 734 us -> 226 us  [the longest x2 141 us: fetch_items(): lax.all_to_all(local_items, 'node', split_axis=2, concat_axis=0, tiled=True)]
    gather x7 -> x4, local copies, waits for them, and re-layouts: 33.3 us -> 8.34 us  [the longest x2 6.44 us: fetch_items(): picked = jnp.take(spread, wanted, axis=0)]
    mul x2 -> x0, other arithmetic: 23.4 us -> none  [pack_items(): return picked * present.astype(local_items.dtype)[:, None, None, None]]
    all_to_all x0 -> x5, local copies, waits for them, and re-layouts: none -> 13.8 us  [the longest x3 11.8 us: fetch_items(): lax.all_to_all(local_items, 'node', split_axis=2, concat_axis=0, tiled=True)]
    all_to_all x2 -> x4, starting transfers between devices: 11.5 us -> 20.3 us  [the longest x2 11.5 us: fetch_items(): lax.all_to_all(local_items, 'node', split_axis=2, concat_axis=0, tiled=True)]
  transfers between devices with their start and end apart: 2 -> 4, of which waited for: 2 -> 4; matrix products, arithmetic and copies ran while one was open for 1% -> 4% of each run, Pallas kernels for 0% -> 0%
where the time goes in v1:
time: 309 us; the launch traced here: 308 us
  waiting for transfers between devices  226 us (73%)
  local copies, waits for them, and re-layouts  43.7 us (14%)
  starting transfers between devices  20.3 us (7%)
  matrix products  10.7 us (3%)
  other arithmetic  7.45 us (2%)
    all_to_all x2, waiting for transfers between devices, fetch_items(): lax.all_to_all(local_items, 'node', split_axis=2, concat_axis=0, tiled=True)  141 us
    all_to_all x2, waiting for transfers between devices, fetch_items(): lax.all_to_all(picked, 'node', split_axis=0, concat_axis=2, tiled=True)  85 us
    all_to_all x3, local copies, waits for them, and re-layouts, fetch_items(): lax.all_to_all(local_items, 'node', split_axis=2, concat_axis=0, tiled=True)  11.8 us
    all_to_all x2, starting transfers between devices, fetch_items(): lax.all_to_all(local_items, 'node', split_axis=2, concat_axis=0, tiled=True)  11.5 us
    all_to_all x2, starting transfers between devices, fetch_items(): lax.all_to_all(picked, 'node', split_axis=0, concat_axis=2, tiled=True)  8.73 us
    unnamed x15, local copies, waits for them, and re-layouts  7.8 us
    dot_general x2, matrix products, complex_product(): jnp.einsum('jmk,jkn->jmn', stacked_left, stacked_right, precision=lax.Pre...  7.48 us
    gather x2, local copies, waits for them, and re-layouts, fetch_items(): picked = jnp.take(spread, wanted, axis=0)  6.44 us
  transfers between devices with their start and end apart: 4, of which 4 were waited for; matrix products, arithmetic and copies ran while one was open for 4% of the time, Pallas kernels for 0%

profile of v1, /device:TPU:0, one launch (start us, length us, event | category | flops | bytes accessed | tf_op | source)
XLA Modules:
  0.0 308.4 jit_solution(6629848441954588544)
XLA Ops:
  0.0 6.6 %copy.51 = f32[8,2,256,256]{3,0,1,2:T(8,128)} copy(f32[8,2,256,256]{3,2,1,0:T(8,128)} %param.6) | data formatting | bytes 8388608 | tf_op args[0]
  6.6 7.5 %all-to-all-start = ((f32[8,2,256,256]{3,0,1,2:T(8,128)}), f32[8,2,256,256]{3,0,1,2:T(8,128)}, u32[]{:S(2)}, u32[]{:S(2)}) async-start(f32[8,2,256,256]{3,0,1,2:T(8,128)} %copy.51), calls=%async_computation | async-start | bytes 8388608 | tf_op jit(solution)/shard_map/all_to_all | solution.py:26
  14.1 1.3 gather_fusion.2
  15.5 92.3 %all-to-all-done = f32[8,2,256,256]{3,0,1,2:T(8,128)} async-done(((f32[8,2,256,256]{3,0,1,2:T(8,128)}), f32[8,2,256,256]{3,0,1,2:T(8,128)}, u32[]{:S(2)}, u32[]{:S(2)}) %all-to-all-start) | async-done | bytes 4194336 | tf_op jit(solution)/shard_map/all_to_all | solution.py:26
  107.8 8.0 %copy.53 = f32[32,8,2,8,256]{4,3,2,1,0:T(8,128)} copy(f32[32,8,2,8,256]{4,1,2,3,0:T(8,128)} %bitcast.11) | data formatting | bytes 8388608 | tf_op jit(solution)/shard_map/all_to_all | solution.py:26
  115.8 2.9 gather_fusion.3
  118.7 1.5 broadcast_select_fusion.1
  120.2 4.3 %all-to-all-start.1 = ((f32[128,2,8,256]{3,2,1,0:T(8,128)}), f32[128,2,8,256]{3,2,1,0:T(8,128)S(1)}, u32[]{:S(2)}, u32[]{:S(2)}) async-start(f32[128,2,8,256]{3,2,1,0:T(8,128)} %broadcast_select_fusion.1), calls=%async_computation.1 | async-start | bytes 4194304 | tf_op jit(solution)/shard_map/all_to_all | solution.py:28
  124.6 0.6 gather_fusion
  125.3 4.2 %gather_fusion.1 = f32[4,2,256,256]{3,2,1,0:T(8,128)} fusion(f32[8,2,256,256]{3,2,1,0:T(8,128)} %param.6, s32[1024]{0:T(1024)S(1)} %pad_clamp_fusion.4), kind=kCustom, calls=%fused_computation.1 | custom fusion | bytes 4194320 | tf_op jit(solution)/shard_map/jit(_take)/gather | solution.py:41
  129.4 1.8 copy_select_fusion.1
  131.3 1.1 slice_bitcast_fusion.11
  132.4 40.8 %all-to-all-done.1 = f32[128,2,8,256]{3,2,1,0:T(8,128)S(1)} async-done(((f32[128,2,8,256]{3,2,1,0:T(8,128)}), f32[128,2,8,256]{3,2,1,0:T(8,128)S(1)}, u32[]{:S(2)}, u32[]{:S(2)}) %all-to-all-start.1) | async-done | bytes 2097184 | tf_op jit(solution)/shard_map/all_to_all | solution.py:28
  173.6 1.1 copy-done.2
  174.7 3.7 %fusion = f32[4,256,512]{2,1,0:T(8,128)S(1)} fusion(f32[4,256,256]{2,1,0:T(8,128)S(1)} %get-tuple-element.18, f32[4,256,256]{2,1,0:T(8,128)S(1)} %get-tuple-element.17, f32[4,256,256]{2,1,0:T(8,128)S(1)} %fusion.35, f32[4,256,256]{2,1,0:T(8,128)S(1)} %copy-done.2, f32[4,256,256]{2,1,0:T(8,128)S(1)} %get-tuple-element.15), kind=kOutput, calls=%fused_computation.6 | convolution fusion | flops 3224895488 | bytes 7340032 | tf_op jit(solution)/shard_map/jmk,jkn->jmn/dot_general | solution.py:15
  178.8 2.7 copy.57
  181.5 4.1 %all-to-all-start.2 = ((f32[4,2,256,256]{3,0,1,2:T(4,128)}), f32[4,2,256,256]{3,0,1,2:T(4,128)}, u32[]{:S(2)}, u32[]{:S(2)}) async-start(f32[4,2,256,256]{3,0,1,2:T(4,128)} %copy.57), calls=%async_computation.2 | async-start | bytes 4194304 | tf_op jit(solution)/shard_map/all_to_all | solution.py:26
  185.6 48.7 %all-to-all-done.2 = f32[4,2,256,256]{3,0,1,2:T(4,128)} async-done(((f32[4,2,256,256]{3,0,1,2:T(4,128)}), f32[4,2,256,256]{3,0,1,2:T(4,128)}, u32[]{:S(2)}, u32[]{:S(2)}) %all-to-all-start.2) | async-done | bytes 2097184 | tf_op jit(solution)/shard_map/all_to_all | solution.py:26
  234.3 2.3 copy.73
  236.5 1.6 copy.59
  238.1 3.6 %gather_fusion.5 = f32[128,2,8,256]{3,2,1,0:T(8,128)} fusion(f32[128,2,8,256]{3,2,1,0:T(8,128)} %bitcast.80, s32[1024]{0:T(1024)S(1)} %pad_clamp_fusion), kind=kCustom, calls=%fused_computation.5 | custom fusion | bytes 4194816 | tf_op jit(solution)/shard_map/jit(_take)/gather | solution.py:27
  241.7 3.1 %broadcast_select_fusion = f32[128,2,8,256]{3,2,1,0:T(8,128)} fusion(f32[128,2,8,256]{3,2,1,0:T(8,128)} %gather_fusion.5, pred[128]{0:T(512)(128)(4,1)S(1)} %and_bitcast_fusion), kind=kLoop, calls=%fused_computation.49 | loop fusion | flops 524288 | bytes 4194432 | tf_op jit(solution)/shard_map/jit(_take)/select_n | solution.py:27
  244.8 4.4 %all-to-all-start.3 = ((f32[128,2,8,256]{3,2,1,0:T(8,128)}), f32[128,2,8,256]{3,2,1,0:T(8,128)}, u32[]{:S(2)}, u32[]{:S(2)}) async-start(f32[128,2,8,256]{3,2,1,0:T(8,128)} %broadcast_select_fusion), calls=%async_computation.3 | async-start | bytes 4194304 | tf_op jit(solution)/shard_map/all_to_all | solution.py:28
  249.5 1.6 copy.55
  251.0 2.3 gather_fusion.4
  253.3 0.2 copy_select_fusion
  253.7 44.2 %all-to-all-done.3 = f32[128,2,8,256]{3,2,1,0:T(8,128)} async-done(((f32[128,2,8,256]{3,2,1,0:T(8,128)}), f32[128,2,8,256]{3,2,1,0:T(8,128)}, u32[]{:S(2)}, u32[]{:S(2)}) %all-to-all-start.3) | async-done | bytes 2097184 | tf_op jit(solution)/shard_map/all_to_all | solution.py:28
  297.9 1.8 copy.72
  299.9 3.7 %fusion.8 = f32[4,256,512]{2,1,0:T(8,128)S(1)} fusion(f32[4,256,256]{2,1,0:T(8,128)S(1)} %get-tuple-element.12, f32[4,256,256]{2,1,0:T(8,128)S(1)} %get-tuple-element.11, f32[4,256,256]{2,1,0:T(8,128)S(1)} %fusion.36, f32[4,256,256]{2,1,0:T(8,128)S(1)} %get-tuple-element.10, f32[4,256,256]{2,1,0:T(8,128)S(1)} %get-tuple-element.9), kind=kOutput, calls=%fused_computation.14 | convolution fusion | flops 3224895488 | bytes 7340032 | tf_op jit(solution)/shard_map/jmk,jkn->jmn/dot_general | solution.py:15
  303.8 0.2 maximum_multiply_fusion
  304.1 3.2 %fusion.22 = f32[2,2,256,256]{3,0,2,1:T(2,128)S(1)} fusion(f32[4,2,256,256]{3,2,0,1:T(8,128)S(1)} %maximum_multiply_fusion, s32[4]{0:T(128)S(1)} %get-tuple-element.20), kind=kOutput, calls=%fused_computation.30 | convolution fusion | flops 12582920 | bytes 3145744 | tf_op jit(solution)/shard_map/rj,jxmn->rxmn/dot_general | solution.py:51
  307.4 1.1 copy.62
  (40 shorter events, 1.6 us)
Async XLA Ops:
  0.0 14.1 %copy-start = (s32[256]{0:T(256)S(1)}, s32[256]{0:T(256)}, u32[]{:S(2)}) copy-start(s32[256]{0:T(256)} %param.7) | copy-start | bytes 3076
  6.6 7.5 %copy-start.3 = (s32[128,2]{0,1:T(2,128)S(1)}, s32[128,2]{0,1:T(2,128)}, u32[]{:S(2)}) copy-start(s32[128,2]{0,1:T(2,128)} %param.8) | copy-start | bytes 3076
  6.6 101.2 %all-to-all-start = ((f32[8,2,256,256]{3,0,1,2:T(8,128)}), f32[8,2,256,256]{3,0,1,2:T(8,128)}, u32[]{:S(2)}, u32[]{:S(2)}) async-start(f32[8,2,256,256]{3,0,1,2:T(8,128)} %copy.51), calls=%async_computation | async-start | bytes 8388608 | tf_op jit(solution)/shard_map/all_to_all | solution.py:26
  120.2 53.0 %all-to-all-start.1 = ((f32[128,2,8,256]{3,2,1,0:T(8,128)}), f32[128,2,8,256]{3,2,1,0:T(8,128)S(1)}, u32[]{:S(2)}, u32[]{:S(2)}) async-start(f32[128,2,8,256]{3,2,1,0:T(8,128)} %broadcast_select_fusion.1), calls=%async_computation.1 | async-start | bytes 4194304 | tf_op jit(solution)/shard_map/all_to_all | solution.py:28
  173.5 1.2 copy-start.2
  181.5 4.1 %copy-start.4 = (s32[128,2]{0,1:T(2,128)S(1)}, s32[128,2]{0,1:T(2,128)}, u32[]{:S(2)}) copy-start(s32[128,2]{0,1:T(2,128)} %param.9) | copy-start | bytes 3076
  181.5 52.8 %all-to-all-start.2 = ((f32[4,2,256,256]{3,0,1,2:T(4,128)}), f32[4,2,256,256]{3,0,1,2:T(4,128)}, u32[]{:S(2)}, u32[]{:S(2)}) async-start(f32[4,2,256,256]{3,0,1,2:T(4,128)} %copy.57), calls=%async_computation.2 | async-start | bytes 4194304 | tf_op jit(solution)/shard_map/all_to_all | solution.py:26
  244.8 4.5 %copy-start.5 = (s32[128]{0:T(128)S(1)}, s32[128]{0:T(128)}, u32[]{:S(2)}) copy-start(s32[128]{0:T(128)} %param.11) | copy-start | bytes 1540
  244.8 4.5 %copy-start.6 = (s32[128]{0:T(128)S(1)}, s32[128]{0:T(128)}, u32[]{:S(2)}) copy-start(s32[128]{0:T(128)} %param.10) | copy-start | bytes 1540
  244.8 53.1 %all-to-all-start.3 = ((f32[128,2,8,256]{3,2,1,0:T(8,128)}), f32[128,2,8,256]{3,2,1,0:T(8,128)}, u32[]{:S(2)}, u32[]{:S(2)}) async-start(f32[128,2,8,256]{3,2,1,0:T(8,128)} %broadcast_select_fusion), calls=%async_computation.3 | async-start | bytes 4194304 | tf_op jit(solution)/shard_map/all_to_all | solution.py:28
  304.1 4.3 %copy-start.1 = (s32[256]{0:T(256)S(1)}, s32[256]{0:T(256)}, u32[]{:S(2)}) copy-start(s32[256]{0:T(256)} %param.7) | copy-start | bytes 3076

commit v2 on v1

v2 whole, which is shorter than its diff:
```python
import functools

import jax
import jax.numpy as jnp
from jax import lax
from jax.experimental import pallas as pl
from jax.experimental.pallas import tpu as pltpu
from jax.sharding import PartitionSpec as P

RES_COL = 2
LANES = 128
NODE_SHARE = 9 / 32
PAIR_SHARE = 0.5
ANY = pl.BlockSpec(memory_space=pl.ANY)
SMEM = pl.BlockSpec(memory_space=pltpu.SMEM)
VMEM = pl.BlockSpec(memory_space=pltpu.VMEM)


def cut_kernel(in_ref, out_ref):
    rows = out_ref.shape[3]
    for j in range(out_ref.shape[0]):
        out_ref[j] = in_ref[:, :, j * rows : (j + 1) * rows, :]


def cut_rows(nodes, group, part, width):
    count, _, order, _ = nodes.shape
    rows = order // group
    steps = 4 if group % 4 == 0 else 1
    return pl.pallas_call(
        cut_kernel,
        grid=(steps,),
        in_specs=[pl.BlockSpec((count, 2, order // steps, width), lambda i: (0, 0, i, part))],
        out_specs=pl.BlockSpec((group // steps, count, 2, rows, width), lambda i: (i, 0, 0, 0, 0)),
        out_shape=jax.ShapeDtypeStruct((group, count, 2, rows, width), jnp.float32),
        name="cut_rows",
    )(nodes)


def cross_kernel(skip, half_ref, ids_ref, spread_ref, out_ref, seen_ref, sem):
    half = half_ref[0]
    count, room = spread_ref.shape[0], out_ref.shape[0]
    asked = ids_ref.shape[0] // 2

    def clear(i, carry):
        seen_ref[i] = 0
        return carry

    lax.fori_loop(0, count, clear, 0, unroll=8)

    def visit(q, found):
        item = ids_ref[(1 - half) * asked + q] - half * count
        inside = (item >= 0) & (item < count)
        safe = jnp.where(inside, item, 0)
        fresh = inside & (seen_ref[safe] == 0)
        place = found - skip

        @pl.when(fresh)
        def _():
            seen_ref[safe] = 1

        @pl.when(fresh & (place >= 0) & (place < room))
        def _():
            pltpu.make_async_copy(spread_ref.at[safe], out_ref.at[place], sem).start()

        return found + fresh.astype(jnp.int32)

    found = lax.fori_loop(0, asked, visit, jnp.int32(0))

    def fill(i, carry):
        pltpu.make_async_copy(spread_ref.at[0], out_ref.at[i], sem).start()
        return carry

    lax.fori_loop(jnp.clip(found - skip, 0, room), room, fill, 0)
    pltpu.make_async_copy(spread_ref.at[pl.ds(0, room)], out_ref, sem).wait()


def pick_cross(half, ids, spread, skip, room):
    return pl.pallas_call(
        functools.partial(cross_kernel, skip),
        in_specs=[SMEM, SMEM, ANY],
        out_specs=VMEM,
        out_shape=jax.ShapeDtypeStruct((room,) + spread.shape[1:], jnp.float32),
        scratch_shapes=[pltpu.SMEM((spread.shape[0],), jnp.int32), pltpu.SemaphoreType.DMA],
        name="pick_cross",
    )(half, ids, spread)


def own_kernel(half_ref, ids_ref, spread_ref, recv_ref, extra_ref, out_ref, place_ref, sem):
    half = half_ref[0]
    count, room = spread_ref.shape[0], recv_ref.shape[0]
    asked = out_ref.shape[0]

    def clear(i, carry):
        place_ref[i] = -1
        return carry

    lax.fori_loop(0, count, clear, 0, unroll=8)

    def visit(q, found):
        item = ids_ref[half * asked + q]
        here = item - half * count
        there = item - (1 - half) * count
        inside = (here >= 0) & (here < count)

        @pl.when(inside)
        def _():
            pltpu.make_async_copy(spread_ref.at[here], out_ref.at[q], sem).start()

        safe = jnp.where(inside, 0, there)
        known = place_ref[safe]
        fresh = (known < 0) & jnp.logical_not(inside)
        place = jnp.where(known < 0, found, known)

        @pl.when(fresh)
        def _():
            place_ref[safe] = found

        @pl.when(jnp.logical_not(inside) & (place < room))
        def _():
            pltpu.make_async_copy(recv_ref.at[place], out_ref.at[q], sem).start()

        @pl.when(jnp.logical_not(inside) & (place >= room))
        def _():
            pltpu.make_async_copy(extra_ref.at[place - room], out_ref.at[q], sem).start()

        return found + fresh.astype(jnp.int32)

    lax.fori_loop(0, asked, visit, jnp.int32(0))
    pltpu.make_async_copy(spread_ref.at[pl.ds(0, asked)], out_ref, sem).wait()


def pick_own(half, ids, spread, recv, extra):
    asked = ids.shape[0] // 2
    return pl.pallas_call(
        own_kernel,
        in_specs=[SMEM, SMEM, ANY, ANY, ANY],
        out_specs=VMEM,
        out_shape=jax.ShapeDtypeStruct((asked,) + spread.shape[1:], jnp.float32),
        scratch_shapes=[pltpu.SMEM((spread.shape[0],), jnp.int32), pltpu.SemaphoreType.DMA],
        name="pick_own",
    )(half, ids, spread, recv, extra)


def most_crossing(ids, count):
    asked = ids.shape[0] // 2
    items = jnp.arange(2 * count, dtype=jnp.int32)
    hits = (ids.reshape(2, asked, 1) == items).any(axis=1)
    crossing = hits & (items // count != jnp.arange(2, dtype=jnp.int32)[:, None])
    return jnp.max(jnp.sum(crossing.astype(jnp.int32), axis=1))


def fetch_items(parts, ids, share):
    devices = lax.axis_size("node")
    group = devices // 2
    half = (lax.axis_index("node") // group).astype(jnp.int32).reshape(1)
    halves = [[h * group + i for i in range(group)] for h in range(2)]
    swap = [(i, (i + group) % devices) for i in range(devices)]
    count = group * parts[0].shape[1]
    room = min(count, max(8, int(count * share)))
    crowded = most_crossing(ids, count) > room
    fetched = []
    for part in parts:
        spread = lax.all_to_all(part, "node", 0, 0, axis_index_groups=halves, tiled=True)
        spread = spread.reshape((count,) + spread.shape[2:])
        recv = lax.ppermute(pick_cross(half, ids, spread, 0, room), "node", swap)
        rest = count - room
        if rest:
            extra = lax.cond(
                crowded,
                lambda x: lax.ppermute(pick_cross(half, ids, x, room, rest), "node", swap),
                lambda x: jnp.zeros((rest,) + x.shape[1:], x.dtype),
                spread,
            )
        else:
            extra = recv
        picked = pick_own(half, ids, spread, recv, extra)
        picked = picked.reshape((group, picked.shape[0] // group) + picked.shape[1:])
        fetched.append(
            lax.all_to_all(picked, "node", 0, 0, axis_index_groups=halves, tiled=True)
        )
    return fetched


def joined(left_real, left_imag, right):
    order = left_real.shape[1]
    width = right.shape[-1]
    right_real = right[:, 0, 0].reshape(order, width)
    right_imag = right[:, 0, 1].reshape(order, width)
    stacked_left = jnp.concatenate([left_real, left_imag], axis=1)
    stacked_right = jnp.concatenate(
        [
            jnp.concatenate([right_real, right_imag], axis=1),
            jnp.concatenate([-right_imag, right_real], axis=1),
        ],
        axis=0,
    )
    return jnp.dot(
        stacked_left,
        stacked_right,
        precision=lax.Precision.HIGHEST,
        preferred_element_type=jnp.float32,
    )


def pair_kernel(first_ref, left_ref, right_ref, out_ref):
    group, _, _, rows, width = out_ref.shape
    both = joined(left_ref[0, 0], left_ref[0, 1], right_ref[...])
    out_ref[:, 0, 0] = both[:, :width].reshape(group, rows, width)
    out_ref[:, 0, 1] = both[:, width:].reshape(group, rows, width)


def pair_products(first_slot, nodes, right):
    group, pairs, _, rows, width = right.shape
    block = (group, 1, 2, rows, width)
    order = nodes.shape[2]
    return pl.pallas_call(
        pair_kernel,
        grid_spec=pltpu.PrefetchScalarGridSpec(
            num_scalar_prefetch=1,
            grid=(pairs,),
            in_specs=[
                pl.BlockSpec((1, 2, order, order), lambda k, first: (first[k], 0, 0, 0)),
                pl.BlockSpec(block, lambda k, first: (0, k, 0, 0, 0)),
            ],
            out_specs=pl.BlockSpec(block, lambda k, first: (0, k, 0, 0, 0)),
        ),
        out_shape=jax.ShapeDtypeStruct(right.shape, jnp.float32),
        name="pair_products",
    )(first_slot, nodes, right)


def second_kernel(side_count, left_index, target, sign, *refs):
    left_refs, right_ref, out_ref = refs[:side_count], refs[side_count], refs[-1]
    step = pl.program_id(0)
    order = out_ref.shape[2]
    width = right_ref.shape[-1]

    @pl.when(step == 0)
    def _():
        out_ref[...] = jnp.zeros_like(out_ref)

    sides = [
        jnp.concatenate([ref[:, 0, c].reshape(order, ref.shape[-1]) for ref in left_refs], axis=1)
        for c in range(2)
    ]
    both = joined(sides[0], sides[1], right_ref[...]) * sign[step].astype(jnp.float32)
    row = target[step]
    out_ref[row, 0] += both[:, :width]
    out_ref[row, 1] += both[:, width:]


def second_products(left_index, target, sign, lefts, right, part, parts, before):
    group, seconds, _, rows, width = right.shape
    order = group * rows
    block = (group, 1, 2, rows, width)
    left_spec = pl.BlockSpec(block, lambda k, left, t, s: (0, left[k], 0, 0, 0))
    in_specs = [left_spec] * len(lefts)
    in_specs.append(pl.BlockSpec(block, lambda k, left, t, s: (0, k, 0, 0, 0)))
    operands = [left_index, target, sign, *lefts, right]
    aliases = {}
    if before is not None:
        aliases = {len(operands): 0}
        operands.append(before)
        in_specs.append(ANY)
    return pl.pallas_call(
        functools.partial(second_kernel, len(lefts)),
        grid_spec=pltpu.PrefetchScalarGridSpec(
            num_scalar_prefetch=3,
            grid=(seconds,),
            in_specs=in_specs,
            out_specs=pl.BlockSpec(
                (RES_COL, 2, order, width), lambda k, left, t, s: (0, 0, 0, part)
            ),
        ),
        out_shape=jax.ShapeDtypeStruct((RES_COL, 2, order, width * parts), jnp.float32),
        input_output_aliases=aliases,
        name="second_products",
    )(*operands)


def per_device(node_blocks, node_slot, pair_list, second_list, targets, spin_signs):
    devices = lax.axis_size("node")
    column = lax.axis_index("node")
    group = devices // 2
    node_col, _, _, local_width = node_blocks.shape
    pair_col = pair_list.shape[0] // devices
    second_col = second_list.shape[0] // devices
    width = min(LANES, local_width)
    parts = local_width // width
    cuts = [cut_rows(node_blocks, group, c, width) for c in range(parts)]
    rights = fetch_items(cuts, node_slot[pair_list[:, 1]], NODE_SHARE)
    own_pairs = lax.dynamic_slice_in_dim(pair_list, column * pair_col, pair_col, 0)
    first_slot = node_slot[own_pairs[:, 0]] - column * node_col
    whole_nodes = node_blocks
    if lax.axis_size("pair") > 1:
        whole_nodes = lax.all_gather(node_blocks, "pair", axis=3, tiled=True)
    products = [pair_products(first_slot, whole_nodes, right) for right in rights]
    second_rights = fetch_items(products, second_list[:, 1], PAIR_SHARE)
    lefts = products
    if lax.axis_size("pair") > 1:
        gathered = [lax.all_gather(product, "pair", axis=0) for product in products]
        lefts = [g[c] for c in range(lax.axis_size("pair")) for g in gathered]
    own_seconds = lax.dynamic_slice_in_dim(second_list, column * second_col, second_col, 0)
    left_index = own_seconds[:, 0] - column * pair_col
    own_signs = lax.dynamic_slice_in_dim(spin_signs, column * second_col, second_col, 0)
    own_targets = lax.dynamic_slice_in_dim(targets, column * second_col, second_col, 0)
    own_targets = own_targets - column * RES_COL
    results = None
    for part, right in enumerate(second_rights):
        results = second_products(
            left_index, own_targets, own_signs, lefts, right, part, parts, results
        )
    return results


def solution(mesh):
    placed = (P(("cfg", "node"), None, None, "pair"), P(), P(), P(), P(), P())
    return jax.shard_map(
        per_device,
        mesh=mesh,
        in_specs=placed,
        out_specs=P(("cfg", "node"), None, None, "pair"),
        check_vma=False,
    )
```

time: 309 us -> 282 us (0.913)
  waiting for transfers between devices: 226 us -> 157 us
  Pallas kernels: 0 us -> 62.5 us
  local copies, waits for them, and re-layouts: 43.7 us -> 12 us
  starting transfers between devices: 20.3 us -> 44.4 us
  matrix products: 10.7 us -> 0 us
  other arithmetic: 7.45 us -> 3.48 us
    all_to_all x4 -> x8, waiting for transfers between devices: 226 us -> 53.1 us  [the longest x4 35.6 us: fetch_items(): lax.all_to_all(part, 'node', 0, 0, axis_index_groups=halves, tiled=True)]
    ppermute x0 -> x4, waiting for transfers between devices: none -> 103 us  [fetch_items(): recv = lax.ppermute(pick_cross(half, ids, spread, 0, room), 'node', swap)]
    pallas_call x0 -> x14, Pallas kernels: none -> 62.5 us  [the longest x4 16.8 us: pick_own(): pl.pallas_call(own_kernel, in_specs=[SMEM, SMEM, ANY, ANY, ANY], out_spec...]
    all_to_all x4 -> x8, starting transfers between devices: 20.3 us -> 37.9 us  [the longest x4 19.4 us: fetch_items(): lax.all_to_all(picked, 'node', 0, 0, axis_index_groups=halves, tiled=True)]
    all_to_all x5 -> x0, local copies, waits for them, and re-layouts: 13.8 us -> none  [the longest x3 11.8 us: fetch_items(): lax.all_to_all(local_items, 'node', split_axis=2, concat_axis=0, tiled=True)]
    gather x5 -> x1, local copies, waits for them, and re-layouts: 14.1 us -> 1.27 us  [per_device(): rights = fetch_items(cuts, node_slot[pair_list[:, 1]], NODE_SHARE)]
    dot_general x3 -> x0, matrix products: 10.7 us -> none  [the longest x2 7.48 us: complex_product(): jnp.einsum('jmk,jkn->jmn', stacked_left, stacked_right, precision=lax.Pre...]
    select_n x8 -> x3, other arithmetic: 6.76 us -> 0.01 us  [the longest x2 0.01 us: most_crossing(): items // count != jnp.arange(2, dtype=jnp.int32)[:, None]]
  transfers between devices with their start and end apart: 4 -> 12, of which waited for: 4 -> 8; matrix products, arithmetic and copies ran while one was open for 4% -> 4% of each run, Pallas kernels for 0% -> 19%
where the time goes in v2:
time: 282 us; the launch traced here: 281 us
  waiting for transfers between devices  157 us (56%)
  Pallas kernels  62.5 us (22%)
  starting transfers between devices  44.4 us (16%)
  local copies, waits for them, and re-layouts  12 us (4%)
  other arithmetic  3.48 us (1%)
    ppermute x4, waiting for transfers between devices, fetch_items(): recv = lax.ppermute(pick_cross(half, ids, spread, 0, room), 'node', swap)  103 us
    all_to_all x4, waiting for transfers between devices, fetch_items(): lax.all_to_all(part, 'node', 0, 0, axis_index_groups=halves, tiled=True)  35.6 us
    all_to_all x4, starting transfers between devices, fetch_items(): lax.all_to_all(picked, 'node', 0, 0, axis_index_groups=halves, tiled=True)  19.4 us
    all_to_all x4, starting transfers between devices, fetch_items(): lax.all_to_all(part, 'node', 0, 0, axis_index_groups=halves, tiled=True)  18.5 us
    all_to_all x4, waiting for transfers between devices, fetch_items(): lax.all_to_all(picked, 'node', 0, 0, axis_index_groups=halves, tiled=True)  17.6 us
    pallas_call x4, Pallas kernels, pick_own(): pl.pallas_call(own_kernel, in_specs=[SMEM, SMEM, ANY, ANY, ANY], out_spec...  16.8 us
    pallas_call x4, Pallas kernels, pick_cross(): pl.pallas_call(functools.partial(cross_kernel, skip), in_specs=[SMEM, SME...  15.1 us
    pallas_call x2, Pallas kernels, second_products(): pl.pallas_call(functools.partial(second_kernel, len(lefts)), grid_spec=pl...  11.6 us
  transfers between devices with their start and end apart: 12, of which 8 were waited for; matrix products, arithmetic and copies ran while one was open for 4% of the time, Pallas kernels for 19%

profile of v2, /device:TPU:0, one launch (start us, length us, event | category | flops | bytes accessed | tf_op | source)
XLA Modules:
  0.0 280.7 jit_solution(16405505927310686037)
XLA Ops:
  0.0 3.8 %cut_rows.2 = f32[16,8,2,16,128]{4,3,2,1,0:T(8,128)} custom-call(f32[8,2,256,256]{3,2,1,0:T(8,128)} %left_ref.3), custom_call_target="tpu_custom_call" | custom-call | tf_op jit(solution)/shard_map/cut_rows/pallas_call | solution.py:29
  3.8 6.3 %all-to-all-start = ((f32[16,8,2,16,128]{4,3,2,1,0:T(8,128)}), f32[16,8,2,16,128]{4,3,2,1,0:T(8,128)S(1)}, u32[]{:S(2)}, u32[]{:S(2)}) async-start(f32[16,8,2,16,128]{4,3,2,1,0:T(8,128)} %cut_rows.2), calls=%async_computation | async-start | bytes 4194304 | tf_op jit(solution)/shard_map/all_to_all | solution.py:163
  10.1 3.8 %cut_rows.3 = f32[16,8,2,16,128]{4,3,2,1,0:T(8,128)} custom-call(f32[8,2,256,256]{3,2,1,0:T(8,128)} %left_ref.3), custom_call_target="tpu_custom_call" | custom-call | tf_op jit(solution)/shard_map/cut_rows/pallas_call | solution.py:29
  14.0 25.2 %all-to-all-done = f32[16,8,2,16,128]{4,3,2,1,0:T(8,128)S(1)} async-done(((f32[16,8,2,16,128]{4,3,2,1,0:T(8,128)}), f32[16,8,2,16,128]{4,3,2,1,0:T(8,128)S(1)}, u32[]{:S(2)}, u32[]{:S(2)}) %all-to-all-start) | async-done | bytes 2097184 | tf_op jit(solution)/shard_map/all_to_all | solution.py:163
  40.5 4.9 %all-to-all-start.2 = ((f32[16,8,2,16,128]{4,3,2,1,0:T(8,128)}), f32[16,8,2,16,128]{4,3,2,1,0:T(8,128)S(1)}, u32[]{:S(2)}, u32[]{:S(2)}) async-start(f32[16,8,2,16,128]{4,3,2,1,0:T(8,128)} %cut_rows.3), calls=%async_computation.2 | async-start | bytes 4194304 | tf_op jit(solution)/shard_map/all_to_all | solution.py:163
  46.8 3.7 %pick_cross.12 = f32[36,2,16,128]{3,2,1,0:T(8,128)} custom-call(s32[1]{0:T(128)} %bitcast.2.half_ref, s32[128]{0:T(128)S(1)} %gather_fusion.1, f32[128,2,16,128]{3,2,1,0:T(8,128)} %bitcast.20), custom_call_target="tpu_custom_call" | custom-call | tf_op jit(solution)/shard_map/pick_cross/pallas_call | solution.py:78
  50.5 2.3 collective-permute-start.4
  55.7 29.5 %collective-permute-done.4.recv_ref = f32[36,2,16,128]{3,2,1,0:T(8,128)S(1)} collective-permute-done((f32[36,2,16,128]{3,2,1,0:T(8,128)}, f32[36,2,16,128]{3,2,1,0:T(8,128)S(1)}, u32[]{:S(2)}, u32[]{:S(2)}) %collective-permute-start.4) | collective-permute-done | bytes 589856 | tf_op jit(solution)/shard_map/ppermute | solution.py:165
  86.1 3.7 %pick_own.4 = f32[64,2,16,128]{3,2,1,0:T(8,128)} custom-call(s32[1]{0:T(128)} %bitcast.2.half_ref, s32[128]{0:T(128)S(1)} %gather_fusion.1, f32[128,2,16,128]{3,2,1,0:T(8,128)} %bitcast.22, f32[36,2,16,128]{3,2,1,0:T(8,128)} %copy-done.6, f32[92,2,16,128]{3,2,1,0:T(8,128)} %get-tuple-element.55.extra_ref), custom_call_target="tpu_custom_call" | custom-call | tf_op jit(solution)/shard_map/pick_own/pallas_call | solution.py:134
  89.8 7.5 %all-to-all-start.1 = ((f32[16,4,2,16,128]{4,3,2,1,0:T(8,128)}), f32[16,4,2,16,128]{4,3,2,1,0:T(8,128)S(1)}, u32[]{:S(2)}, u32[]{:S(2)}) async-start(f32[16,4,2,16,128]{4,3,2,1,0:T(8,128)} %bitcast.31), calls=%async_computation.1 | async-start | bytes 2097152 | tf_op jit(solution)/shard_map/all_to_all | solution.py:179
  97.3 3.9 %pick_cross.13 = f32[36,2,16,128]{3,2,1,0:T(8,128)} custom-call(s32[1]{0:T(128)} %bitcast.2.half_ref, s32[128]{0:T(128)S(1)} %gather_fusion.1, f32[128,2,16,128]{3,2,1,0:T(8,128)S(1)} %bitcast.17), custom_call_target="tpu_custom_call" | custom-call | tf_op jit(solution)/shard_map/pick_cross/pallas_call | solution.py:78
  102.6 28.2 %collective-permute-done.5.recv_ref = f32[36,2,16,128]{3,2,1,0:T(8,128)} collective-permute-done((f32[36,2,16,128]{3,2,1,0:T(8,128)}, f32[36,2,16,128]{3,2,1,0:T(8,128)}, u32[]{:S(2)}, u32[]{:S(2)}) %collective-permute-start.5) | collective-permute-done | bytes 589856 | tf_op jit(solution)/shard_map/ppermute | solution.py:165
  130.8 4.2 %pick_own.5 = f32[64,2,16,128]{3,2,1,0:T(8,128)} custom-call(s32[1]{0:T(128)} %bitcast.2.half_ref, s32[128]{0:T(128)S(1)} %gather_fusion.1, f32[128,2,16,128]{3,2,1,0:T(8,128)S(1)} %bitcast.19, f32[36,2,16,128]{3,2,1,0:T(8,128)} %collective-permute-done.5.recv_ref, f32[92,2,16,128]{3,2,1,0:T(8,128)} %get-tuple-element.56.extra_ref), custom_call_target="tpu_custom_call" | custom-call | tf_op jit(solution)/shard_map/pick_own/pallas_call | solution.py:134
  135.0 3.9 %all-to-all-start.3 = ((f32[16,4,2,16,128]{4,3,2,1,0:T(8,128)}), f32[16,4,2,16,128]{4,3,2,1,0:T(8,128)S(1)}, u32[]{:S(2)}, u32[]{:S(2)}) async-start(f32[16,4,2,16,128]{4,3,2,1,0:T(8,128)} %bitcast.32), calls=%async_computation.3 | async-start | bytes 2097152 | tf_op jit(solution)/shard_map/all_to_all | solution.py:179
  140.2 5.7 %pair_products.2.refs_0_ = f32[16,4,2,16,128]{4,3,2,1,0:T(8,128)} custom-call(s32[4]{0:T(128)} %broadcast_subtract_fusion.first_ref, f32[8,2,256,256]{3,2,1,0:T(8,128)} %left_ref.3, f32[16,4,2,16,128]{4,3,2,1,0:T(8,128)} %copy-done.2), custom_call_target="tpu_custom_call" | custom-call | tf_op jit(solution)/shard_map/pair_products/pallas_call | solution.py:216
  145.9 9.1 %all-to-all-done.3.right_ref = f32[16,4,2,16,128]{4,3,2,1,0:T(8,128)S(1)} async-done(((f32[16,4,2,16,128]{4,3,2,1,0:T(8,128)}), f32[16,4,2,16,128]{4,3,2,1,0:T(8,128)S(1)}, u32[]{:S(2)}, u32[]{:S(2)}) %all-to-all-start.3) | async-done | bytes 1048608 | tf_op jit(solution)/shard_map/all_to_all | solution.py:179
  155.0 3.7 %all-to-all-start.6 = ((f32[16,4,2,16,128]{4,3,2,1,0:T(8,128)}), f32[16,4,2,16,128]{4,3,2,1,0:T(8,128)S(1)}, u32[]{:S(2)}, u32[]{:S(2)}) async-start(f32[16,4,2,16,128]{4,3,2,1,0:T(8,128)} %pair_products.2.refs_0_), calls=%async_computation.6 | async-start | bytes 2097152 | tf_op jit(solution)/shard_map/all_to_all | solution.py:163
  158.7 5.7 %pair_products.3.refs_1_ = f32[16,4,2,16,128]{4,3,2,1,0:T(8,128)} custom-call(s32[4]{0:T(128)} %broadcast_subtract_fusion.first_ref, f32[8,2,256,256]{3,2,1,0:T(8,128)} %left_ref.3, f32[16,4,2,16,128]{4,3,2,1,0:T(8,128)} %copy-done.4), custom_call_target="tpu_custom_call" | custom-call | tf_op jit(solution)/shard_map/pair_products/pallas_call | solution.py:216
  164.5 10.4 %all-to-all-done.6 = f32[16,4,2,16,128]{4,3,2,1,0:T(8,128)S(1)} async-done(((f32[16,4,2,16,128]{4,3,2,1,0:T(8,128)}), f32[16,4,2,16,128]{4,3,2,1,0:T(8,128)S(1)}, u32[]{:S(2)}, u32[]{:S(2)}) %all-to-all-start.6) | async-done | bytes 1048608 | tf_op jit(solution)/shard_map/all_to_all | solution.py:163
  174.8 3.7 %all-to-all-start.4 = ((f32[16,4,2,16,128]{4,3,2,1,0:T(8,128)}), f32[16,4,2,16,128]{4,3,2,1,0:T(8,128)S(1)}, u32[]{:S(2)}, u32[]{:S(2)}) async-start(f32[16,4,2,16,128]{4,3,2,1,0:T(8,128)} %pair_products.3.refs_1_), calls=%async_computation.4 | async-start | bytes 2097152 | tf_op jit(solution)/shard_map/all_to_all | solution.py:163
  178.5 3.7 %pick_cross.15 = f32[32,2,16,128]{3,2,1,0:T(8,128)} custom-call(s32[1]{0:T(128)} %bitcast.2.half_ref, s32[128]{0:T(128)S(1)} %get-tuple-element.54.ids_ref, f32[64,2,16,128]{3,2,1,0:T(8,128)S(1)} %bitcast.26), custom_call_target="tpu_custom_call" | custom-call | tf_op jit(solution)/shard_map/pick_cross/pallas_call | solution.py:78
  186.4 22.4 %collective-permute-done.7.recv_ref = f32[32,2,16,128]{3,2,1,0:T(8,128)S(1)} collective-permute-done((f32[32,2,16,128]{3,2,1,0:T(8,128)}, f32[32,2,16,128]{3,2,1,0:T(8,128)S(1)}, u32[]{:S(2)}, u32[]{:S(2)}) %collective-permute-start.7) | collective-permute-done | bytes 524320 | tf_op jit(solution)/shard_map/ppermute | solution.py:165
  209.6 4.4 %pick_own.7 = f32[64,2,16,128]{3,2,1,0:T(8,128)} custom-call(s32[1]{0:T(128)} %bitcast.2.half_ref, s32[128]{0:T(128)S(1)} %get-tuple-element.54.ids_ref, f32[64,2,16,128]{3,2,1,0:T(8,128)S(1)} %bitcast.28, f32[32,2,16,128]{3,2,1,0:T(8,128)} %copy-done.7, f32[32,2,16,128]{3,2,1,0:T(8,128)} %get-tuple-element.58.extra_ref), custom_call_target="tpu_custom_call" | custom-call | tf_op jit(solution)/shard_map/pick_own/pallas_call | solution.py:134
  214.1 4.0 %all-to-all-start.7 = ((f32[16,4,2,16,128]{4,3,2,1,0:T(8,128)}), f32[16,4,2,16,128]{4,3,2,1,0:T(8,128)S(1)}, u32[]{:S(2)}, u32[]{:S(2)}) async-start(f32[16,4,2,16,128]{4,3,2,1,0:T(8,128)} %bitcast.29), calls=%async_computation.7 | async-start | bytes 2097152 | tf_op jit(solution)/shard_map/all_to_all | solution.py:179
  218.0 3.7 %pick_cross.14 = f32[32,2,16,128]{3,2,1,0:T(8,128)} custom-call(s32[1]{0:T(128)} %bitcast.2.half_ref, s32[128]{0:T(128)S(1)} %get-tuple-element.54.ids_ref, f32[64,2,16,128]{3,2,1,0:T(8,128)S(1)} %bitcast.23), custom_call_target="tpu_custom_call" | custom-call | tf_op jit(solution)/shard_map/pick_cross/pallas_call | solution.py:78
  221.8 2.5 collective-permute-start.6
  225.1 23.3 %collective-permute-done.6.recv_ref = f32[32,2,16,128]{3,2,1,0:T(8,128)S(1)} collective-permute-done((f32[32,2,16,128]{3,2,1,0:T(8,128)}, f32[32,2,16,128]{3,2,1,0:T(8,128)S(1)}, u32[]{:S(2)}, u32[]{:S(2)}) %collective-permute-start.6) | collective-permute-done | bytes 524320 | tf_op jit(solution)/shard_map/ppermute | solution.py:165
  249.2 4.5 %pick_own.6 = f32[64,2,16,128]{3,2,1,0:T(8,128)} custom-call(s32[1]{0:T(128)} %bitcast.2.half_ref, s32[128]{0:T(128)S(1)} %get-tuple-element.54.ids_ref, f32[64,2,16,128]{3,2,1,0:T(8,128)S(1)} %bitcast.25, f32[32,2,16,128]{3,2,1,0:T(8,128)} %copy-done.8, f32[32,2,16,128]{3,2,1,0:T(8,128)} %get-tuple-element.57.extra_ref), custom_call_target="tpu_custom_call" | custom-call | tf_op jit(solution)/shard_map/pick_own/pallas_call | solution.py:134
  253.8 4.0 %all-to-all-start.5 = ((f32[16,4,2,16,128]{4,3,2,1,0:T(8,128)}), f32[16,4,2,16,128]{4,3,2,1,0:T(8,128)S(1)}, u32[]{:S(2)}, u32[]{:S(2)}) async-start(f32[16,4,2,16,128]{4,3,2,1,0:T(8,128)} %bitcast.30), calls=%async_computation.5 | async-start | bytes 2097152 | tf_op jit(solution)/shard_map/all_to_all | solution.py:179
  259.7 5.8 %second_products.2.refs_3_ = f32[2,2,256,256]{3,2,1,0:T(8,128)} custom-call(s32[4]{0:T(128)} %subtract_bitcast_fusion.left_index, s32[4]{0:T(128)} %dynamic-slice_subtract_fusion.target, s32[4]{0:T(128)} %dynamic_slice.14.sign, f32[16,4,2,16,128]{4,3,2,1,0:T(8,128)} %pair_products.2.refs_0_, f32[16,4,2,16,128]{4,3,2,1,0:T(8,128)} %pair_products.3.refs_1_, ...), custom_call_target="tpu_custom_call" | custom-call | tf_op jit(solution)/shard_map/second_products/pallas_call | solution.py:265
  265.5 8.4 %all-to-all-done.5.refs_2_ = f32[16,4,2,16,128]{4,3,2,1,0:T(8,128)S(1)} async-done(((f32[16,4,2,16,128]{4,3,2,1,0:T(8,128)}), f32[16,4,2,16,128]{4,3,2,1,0:T(8,128)S(1)}, u32[]{:S(2)}, u32[]{:S(2)}) %all-to-all-start.5) | async-done | bytes 1048608 | tf_op jit(solution)/shard_map/all_to_all | solution.py:179
  274.9 5.8 %second_products.3 = f32[2,2,256,256]{3,2,1,0:T(8,128)} custom-call(s32[4]{0:T(128)} %subtract_bitcast_fusion.left_index, s32[4]{0:T(128)} %dynamic-slice_subtract_fusion.target, s32[4]{0:T(128)} %dynamic_slice.14.sign, f32[16,4,2,16,128]{4,3,2,1,0:T(8,128)} %pair_products.2.refs_0_, ...), custom_call_target="tpu_custom_call", output_to_operand_aliasing={{}: (6, {})} | custom-call | tf_op jit(solution)/shard_map/second_products/pallas_call | solution.py:265
  (63 shorter events, 21.6 us)
Async XLA Ops:
  0.0 45.5 %copy-start = (s32[256]{0:T(256)S(1)}, s32[256]{0:T(256)}, u32[]{:S(2)}) copy-start(s32[256]{0:T(256)} %param.15) | copy-start | bytes 3076
  3.8 35.4 %all-to-all-start = ((f32[16,8,2,16,128]{4,3,2,1,0:T(8,128)}), f32[16,8,2,16,128]{4,3,2,1,0:T(8,128)S(1)}, u32[]{:S(2)}, u32[]{:S(2)}) async-start(f32[16,8,2,16,128]{4,3,2,1,0:T(8,128)} %cut_rows.2), calls=%async_computation | async-start | bytes 4194304 | tf_op jit(solution)/shard_map/all_to_all | solution.py:163
  14.0 31.5 %copy-start.9 = (s32[128,2]{0,1:T(2,128)S(1)}, s32[128,2]{0,1:T(2,128)}, u32[]{:S(2)}) copy-start(s32[128,2]{0,1:T(2,128)} %param.16) | copy-start | bytes 3076
  39.2 1.3 copy-start.1
  40.5 49.3 %all-to-all-start.2 = ((f32[16,8,2,16,128]{4,3,2,1,0:T(8,128)}), f32[16,8,2,16,128]{4,3,2,1,0:T(8,128)S(1)}, u32[]{:S(2)}, u32[]{:S(2)}) async-start(f32[16,8,2,16,128]{4,3,2,1,0:T(8,128)} %cut_rows.3), calls=%async_computation.2 | async-start | bytes 4194304 | tf_op jit(solution)/shard_map/all_to_all | solution.py:163
  50.5 34.7 %collective-permute-start.4 = (f32[36,2,16,128]{3,2,1,0:T(8,128)}, f32[36,2,16,128]{3,2,1,0:T(8,128)S(1)}, u32[]{:S(2)}, u32[]{:S(2)}) collective-permute-start(f32[36,2,16,128]{3,2,1,0:T(8,128)} %pick_cross.12), channel_id=1, source_target_pairs={{0,16},{1,17},{2,18},{3,19},{4,20},{5,21},{6,22},{7,23},{8,24},{9,... | collective-permute-start | bytes 1769480 | tf_op jit(solution)/shard_map/ppermute | solution.py:165
  85.2 0.8 copy-start.6
  89.8 45.2 %all-to-all-start.1 = ((f32[16,4,2,16,128]{4,3,2,1,0:T(8,128)}), f32[16,4,2,16,128]{4,3,2,1,0:T(8,128)S(1)}, u32[]{:S(2)}, u32[]{:S(2)}) async-start(f32[16,4,2,16,128]{4,3,2,1,0:T(8,128)} %bitcast.31), calls=%async_computation.1 | async-start | bytes 2097152 | tf_op jit(solution)/shard_map/all_to_all | solution.py:179
  101.2 29.6 %collective-permute-start.5 = (f32[36,2,16,128]{3,2,1,0:T(8,128)}, f32[36,2,16,128]{3,2,1,0:T(8,128)}, u32[]{:S(2)}, u32[]{:S(2)}) collective-permute-start(f32[36,2,16,128]{3,2,1,0:T(8,128)} %pick_cross.13), channel_id=1, source_target_pairs={{0,16},{1,17},{2,18},{3,19},{4,20},{5,21},{6,22},{7,23},{8,24},{9,... | collective-permute-start | bytes 1769480 | tf_op jit(solution)/shard_map/ppermute | solution.py:165
  135.0 5.2 %copy-start.2 = (f32[16,4,2,16,128]{4,3,2,1,0:T(8,128)}, f32[16,4,2,16,128]{4,3,2,1,0:T(8,128)S(1)}, u32[]{:S(2)}) copy-start(f32[16,4,2,16,128]{4,3,2,1,0:T(8,128)S(1)} %all-to-all-done.1.right_ref) | copy-start | bytes 3145732
  135.0 20.1 %all-to-all-start.3 = ((f32[16,4,2,16,128]{4,3,2,1,0:T(8,128)}), f32[16,4,2,16,128]{4,3,2,1,0:T(8,128)S(1)}, u32[]{:S(2)}, u32[]{:S(2)}) async-start(f32[16,4,2,16,128]{4,3,2,1,0:T(8,128)} %bitcast.32), calls=%async_computation.3 | async-start | bytes 2097152 | tf_op jit(solution)/shard_map/all_to_all | solution.py:179
  155.0 3.7 %copy-start.4 = (f32[16,4,2,16,128]{4,3,2,1,0:T(8,128)}, f32[16,4,2,16,128]{4,3,2,1,0:T(8,128)S(1)}, u32[]{:S(2)}) copy-start(f32[16,4,2,16,128]{4,3,2,1,0:T(8,128)S(1)} %all-to-all-done.3.right_ref) | copy-start | bytes 3145732
  155.0 19.8 %all-to-all-start.6 = ((f32[16,4,2,16,128]{4,3,2,1,0:T(8,128)}), f32[16,4,2,16,128]{4,3,2,1,0:T(8,128)S(1)}, u32[]{:S(2)}, u32[]{:S(2)}) async-start(f32[16,4,2,16,128]{4,3,2,1,0:T(8,128)} %pair_products.2.refs_0_), calls=%async_computation.6 | async-start | bytes 2097152 | tf_op jit(solution)/shard_map/all_to_all | solution.py:163
  164.5 14.0 %copy-start.10 = (s32[128,2]{0,1:T(2,128)S(1)}, s32[128,2]{0,1:T(2,128)}, u32[]{:S(2)}) copy-start(s32[128,2]{0,1:T(2,128)} %param.17) | copy-start | bytes 3076
  174.8 39.2 %all-to-all-start.4 = ((f32[16,4,2,16,128]{4,3,2,1,0:T(8,128)}), f32[16,4,2,16,128]{4,3,2,1,0:T(8,128)S(1)}, u32[]{:S(2)}, u32[]{:S(2)}) async-start(f32[16,4,2,16,128]{4,3,2,1,0:T(8,128)} %pair_products.3.refs_1_), calls=%async_computation.4 | async-start | bytes 2097152 | tf_op jit(solution)/shard_map/all_to_all | solution.py:163
  182.2 26.6 %collective-permute-start.7 = (f32[32,2,16,128]{3,2,1,0:T(8,128)}, f32[32,2,16,128]{3,2,1,0:T(8,128)S(1)}, u32[]{:S(2)}, u32[]{:S(2)}) collective-permute-start(f32[32,2,16,128]{3,2,1,0:T(8,128)} %pick_cross.15), channel_id=1, source_target_pairs={{0,16},{1,17},{2,18},{3,19},{4,20},{5,21},{6,22},{7,23},{8,24},{9,... | collective-permute-start | bytes 1572872 | tf_op jit(solution)/shard_map/ppermute | solution.py:165
  208.8 0.8 copy-start.7
  214.1 39.7 %all-to-all-start.7 = ((f32[16,4,2,16,128]{4,3,2,1,0:T(8,128)}), f32[16,4,2,16,128]{4,3,2,1,0:T(8,128)S(1)}, u32[]{:S(2)}, u32[]{:S(2)}) async-start(f32[16,4,2,16,128]{4,3,2,1,0:T(8,128)} %bitcast.29), calls=%async_computation.7 | async-start | bytes 2097152 | tf_op jit(solution)/shard_map/all_to_all | solution.py:179
  221.8 26.7 %collective-permute-start.6 = (f32[32,2,16,128]{3,2,1,0:T(8,128)}, f32[32,2,16,128]{3,2,1,0:T(8,128)S(1)}, u32[]{:S(2)}, u32[]{:S(2)}) collective-permute-start(f32[32,2,16,128]{3,2,1,0:T(8,128)} %pick_cross.14), channel_id=1, source_target_pairs={{0,16},{1,17},{2,18},{3,19},{4,20},{5,21},{6,22},{7,23},{8,24},{9,... | collective-permute-start | bytes 1572872 | tf_op jit(solution)/shard_map/ppermute | solution.py:165
  248.4 0.8 copy-start.8
  253.7 4.1 %copy-start.12 = (s32[128]{0:T(128)S(1)}, s32[128]{0:T(128)}, u32[]{:S(2)}) copy-start(s32[128]{0:T(128)} %param.19) | copy-start | bytes 1540
  253.7 4.7 %copy-start.11 = (s32[128]{0:T(128)S(1)}, s32[128]{0:T(128)}, u32[]{:S(2)}) copy-start(s32[128]{0:T(128)} %param.18) | copy-start | bytes 1540
  253.7 5.9 %copy-start.3 = (f32[16,4,2,16,128]{4,3,2,1,0:T(8,128)}, f32[16,4,2,16,128]{4,3,2,1,0:T(8,128)S(1)}, u32[]{:S(2)}) copy-start(f32[16,4,2,16,128]{4,3,2,1,0:T(8,128)S(1)} %all-to-all-done.7.refs_2_) | copy-start | bytes 3145732
  253.8 20.2 %all-to-all-start.5 = ((f32[16,4,2,16,128]{4,3,2,1,0:T(8,128)}), f32[16,4,2,16,128]{4,3,2,1,0:T(8,128)S(1)}, u32[]{:S(2)}, u32[]{:S(2)}) async-start(f32[16,4,2,16,128]{4,3,2,1,0:T(8,128)} %bitcast.30), calls=%async_computation.5 | async-start | bytes 2097152 | tf_op jit(solution)/shard_map/all_to_all | solution.py:179
  273.9 1.0 copy-start.5

commit v3 on v2

--- a/solution.py
+++ b/solution.py
@@ -6,6 +6,7 @@
 from jax.experimental import pallas as pl
 from jax.experimental.pallas import tpu as pltpu
 from jax.sharding import PartitionSpec as P
+
 
 RES_COL = 2
 LANES = 128
@@ -14,6 +15,7 @@
 ANY = pl.BlockSpec(memory_space=pl.ANY)
 SMEM = pl.BlockSpec(memory_space=pltpu.SMEM)
 VMEM = pl.BlockSpec(memory_space=pltpu.VMEM)
+PARAMS = pltpu.CompilerParams(vmem_limit_bytes=16 * 1024 * 1024)
 
 
 def cut_kernel(in_ref, out_ref):
@@ -36,117 +38,122 @@
     )(nodes)
 
 
-def cross_kernel(skip, half_ref, ids_ref, spread_ref, out_ref, seen_ref, sem):
+def plan_kernel(room, half_ref, ids_ref, send_ref, source_ref, crowded_ref, place_ref):
     half = half_ref[0]
-    count, room = spread_ref.shape[0], out_ref.shape[0]
-    asked = ids_ref.shape[0] // 2
+    count = send_ref.shape[0]
+    asked = source_ref.shape[0]
 
     def clear(i, carry):
-        seen_ref[i] = 0
+        place_ref[i] = -1
+        send_ref[i % count] = 0
         return carry
 
-    lax.fori_loop(0, count, clear, 0, unroll=8)
-
-    def visit(q, found):
-        item = ids_ref[(1 - half) * asked + q] - half * count
-        inside = (item >= 0) & (item < count)
-        safe = jnp.where(inside, item, 0)
-        fresh = inside & (seen_ref[safe] == 0)
-        place = found - skip
+    lax.fori_loop(0, 2 * count, clear, 0, unroll=8)
+
+    def visit_other(q, found):
+        item = ids_ref[(1 - half) * asked + q]
+        here = item - half * count
+        inside = (here >= 0) & (here < count)
+        fresh = inside & (place_ref[item] < 0)
 
         @pl.when(fresh)
         def _():
-            seen_ref[safe] = 1
-
-        @pl.when(fresh & (place >= 0) & (place < room))
-        def _():
-            pltpu.make_async_copy(spread_ref.at[safe], out_ref.at[place], sem).start()
+            place_ref[item] = found
+            send_ref[found] = here
 
         return found + fresh.astype(jnp.int32)
 
-    found = lax.fori_loop(0, asked, visit, jnp.int32(0))
-
-    def fill(i, carry):
-        pltpu.make_async_copy(spread_ref.at[0], out_ref.at[i], sem).start()
+    def visit_own(q, found):
+        item = ids_ref[half * asked + q]
+        here = item - half * count
+        inside = (here >= 0) & (here < count)
+        known = place_ref[item]
+        fresh = jnp.logical_not(inside) & (known < 0)
+
+        @pl.when(fresh)
+        def _():
+            place_ref[item] = found
+
+        place = jnp.where(known < 0, found, known)
+        source_ref[q] = jnp.where(inside, here, count + place)
+        return found + fresh.astype(jnp.int32)
+
+    sent = lax.fori_loop(0, asked, visit_other, jnp.int32(0))
+    received = lax.fori_loop(0, asked, visit_own, jnp.int32(0))
+    crowded_ref[0] = (jnp.maximum(sent, received) > room).astype(jnp.int32)
+
+
+def make_plan(half, ids, count, room):
+    asked = ids.shape[0] // 2
+    return pl.pallas_call(
+        functools.partial(plan_kernel, room),
+        in_specs=[SMEM, SMEM],
+        out_specs=[SMEM, SMEM, SMEM],
+        out_shape=[
+            jax.ShapeDtypeStruct((count,), jnp.int32),
+            jax.ShapeDtypeStruct((asked,), jnp.int32),
+            jax.ShapeDtypeStruct((1,), jnp.int32),
+        ],
+        scratch_shapes=[pltpu.SMEM((2 * count,), jnp.int32)],
+        compiler_params=PARAMS,
+        name="make_plan",
+    )(half, ids)
+
+
+def cross_kernel(skip, send_ref, spread_ref, out_ref):
+    def copy(i, carry):
+        out_ref[i] = spread_ref[send_ref[skip + i]]
         return carry
 
-    lax.fori_loop(jnp.clip(found - skip, 0, room), room, fill, 0)
-    pltpu.make_async_copy(spread_ref.at[pl.ds(0, room)], out_ref, sem).wait()
-
-
-def pick_cross(half, ids, spread, skip, room):
+    lax.fori_loop(0, out_ref.shape[0], copy, 0, unroll=4)
+
+
+def pick_cross(send, spread, skip, room):
     return pl.pallas_call(
         functools.partial(cross_kernel, skip),
-        in_specs=[SMEM, SMEM, ANY],
+        in_specs=[SMEM, VMEM],
         out_specs=VMEM,
         out_shape=jax.ShapeDtypeStruct((room,) + spread.shape[1:], jnp.float32),
-        scratch_shapes=[pltpu.SMEM((spread.shape[0],), jnp.int32), pltpu.SemaphoreType.DMA],
+        compiler_params=PARAMS,
         name="pick_cross",
-    )(half, ids, spread)
-
-
-def own_kernel(half_ref, ids_ref, spread_ref, recv_ref, extra_ref, out_ref, place_ref, sem):
-    half = half_ref[0]
+    )(send, spread)
+
+
+def own_kernel(source_ref, spread_ref, recv_ref, extra_ref, out_ref, sem):
     count, room = spread_ref.shape[0], recv_ref.shape[0]
-    asked = out_ref.shape[0]
-
-    def clear(i, carry):
-        place_ref[i] = -1
+
+    def copy(q, carry):
+        source = source_ref[q]
+
+        @pl.when(source < count)
+        def _():
+            out_ref[q] = spread_ref[source]
+
+        @pl.when((source >= count) & (source < count + room))
+        def _():
+            out_ref[q] = recv_ref[source - count]
+
+        @pl.when(source >= count + room)
+        def _():
+            late = pltpu.make_async_copy(extra_ref.at[source - count - room], out_ref.at[q], sem)
+            late.start()
+            late.wait()
+
         return carry
 
-    lax.fori_loop(0, count, clear, 0, unroll=8)
-
-    def visit(q, found):
-        item = ids_ref[half * asked + q]
-        here = item - half * count
-        there = item - (1 - half) * count
-        inside = (here >= 0) & (here < count)
-
-        @pl.when(inside)
-        def _():
-            pltpu.make_async_copy(spread_ref.at[here], out_ref.at[q], sem).start()
-
-        safe = jnp.where(inside, 0, there)
-        known = place_ref[safe]
-        fresh = (known < 0) & jnp.logical_not(inside)
-        place = jnp.where(known < 0, found, known)
-
-        @pl.when(fresh)
-        def _():
-            place_ref[safe] = found
-
-        @pl.when(jnp.logical_not(inside) & (place < room))
-        def _():
-            pltpu.make_async_copy(recv_ref.at[place], out_ref.at[q], sem).start()
-
-        @pl.when(jnp.logical_not(inside) & (place >= room))
-        def _():
-            pltpu.make_async_copy(extra_ref.at[place - room], out_ref.at[q], sem).start()
-
-        return found + fresh.astype(jnp.int32)
-
-    lax.fori_loop(0, asked, visit, jnp.int32(0))
-    pltpu.make_async_copy(spread_ref.at[pl.ds(0, asked)], out_ref, sem).wait()
-
-
-def pick_own(half, ids, spread, recv, extra):
-    asked = ids.shape[0] // 2
+    lax.fori_loop(0, out_ref.shape[0], copy, 0)
+
+
+def pick_own(source, spread, recv, extra):
     return pl.pallas_call(
         own_kernel,
-        in_specs=[SMEM, SMEM, ANY, ANY, ANY],
+        in_specs=[SMEM, VMEM, VMEM, ANY],
         out_specs=VMEM,
-        out_shape=jax.ShapeDtypeStruct((asked,) + spread.shape[1:], jnp.float32),
-        scratch_shapes=[pltpu.SMEM((spread.shape[0],), jnp.int32), pltpu.SemaphoreType.DMA],
+        out_shape=jax.ShapeDtypeStruct((source.shape[0],) + spread.shape[1:], jnp.float32),
+        scratch_shapes=[pltpu.SemaphoreType.DMA],
+        compiler_params=PARAMS,
         name="pick_own",
-    )(half, ids, spread, recv, extra)
-
-
-def most_crossing(ids, count):
-    asked = ids.shape[0] // 2
-    items = jnp.arange(2 * count, dtype=jnp.int32)
-    hits = (ids.reshape(2, asked, 1) == items).any(axis=1)
-    crossing = hits & (items // count != jnp.arange(2, dtype=jnp.int32)[:, None])
-    return jnp.max(jnp.sum(crossing.astype(jnp.int32), axis=1))
+    )(source, spread, recv, extra)
 
 
 def fetch_items(parts, ids, share):
@@ -156,28 +163,25 @@
     halves = [[h * group + i for i in range(group)] for h in range(2)]
     swap = [(i, (i + group) % devices) for i in range(devices)]
     count = group * parts[0].shape[1]
-    room = min(count, max(8, int(count * share)))
-    crowded = most_crossing(ids, count) > room
+    room = min(count - 1, max(8, int(count * share)))
+    rest = count - room
+    send, source, crowded = make_plan(half, ids, count, room)
     fetched = []
     for part in parts:
         spread = lax.all_to_all(part, "node", 0, 0, axis_index_groups=halves, tiled=True)
         spread = spread.reshape((count,) + spread.shape[2:])
-        recv = lax.ppermute(pick_cross(half, ids, spread, 0, room), "node", swap)
-        rest = count - room
-        if rest:
-            extra = lax.cond(
-                crowded,
-                lambda x: lax.ppermute(pick_cross(half, ids, x, room, rest), "node", swap),
-                lambda x: jnp.zeros((rest,) + x.shape[1:], x.dtype),
-                spread,
-            )
-        else:
-            extra = recv
-        picked = pick_own(half, ids, spread, recv, extra)
+        leaving = pick_cross(send, spread, 0, room)
+        recv = lax.ppermute(leaving, "node", swap)
+        extra = lax.cond(
+            crowded[0] > 0,
+            lambda x, s: lax.ppermute(pick_cross(s, x, room, rest), "node", swap),
+            lambda x, s: jnp.zeros((rest,) + x.shape[1:], x.dtype),
+            spread,
+            send,
+        )
+        picked = pick_own(source, spread, recv, extra)
         picked = picked.reshape((group, picked.shape[0] // group) + picked.shape[1:])
-        fetched.append(
-            lax.all_to_all(picked, "node", 0, 0, axis_index_groups=halves, tiled=True)
-        )
+        fetched.append(lax.all_to_all(picked, "node", 0, 0, axis_index_groups=halves, tiled=True))
     return fetched
 
 
@@ -202,9 +206,21 @@
     )
 
 
-def pair_kernel(first_ref, left_ref, right_ref, out_ref):
+def pair_kernel(first_ref, nodes_ref, right_ref, out_ref, left_ref, sems):
     group, _, _, rows, width = out_ref.shape
-    both = joined(left_ref[0, 0], left_ref[0, 1], right_ref[...])
+    step = pl.program_id(0)
+
+    def fetch(k):
+        return pltpu.make_async_copy(nodes_ref.at[first_ref[k]], left_ref.at[k], sems.at[k])
+
+    @pl.when(step == 0)
+    def _():
+        for k in range(left_ref.shape[0]):
+            fetch(k).start()
+
+    fetch(step).wait()
+    left = left_ref[step]
+    both = joined(left[0], left[1], right_ref[...])
     out_ref[:, 0, 0] = both[:, :width].reshape(group, rows, width)
     out_ref[:, 0, 1] = both[:, width:].reshape(group, rows, width)
 
@@ -219,12 +235,17 @@
             num_scalar_prefetch=1,
             grid=(pairs,),
             in_specs=[
-                pl.BlockSpec((1, 2, order, order), lambda k, first: (first[k], 0, 0, 0)),
+                pl.BlockSpec(memory_space=pltpu.HBM),
                 pl.BlockSpec(block, lambda k, first: (0, k, 0, 0, 0)),
             ],
             out_specs=pl.BlockSpec(block, lambda k, first: (0, k, 0, 0, 0)),
+            scratch_shapes=[
+                pltpu.VMEM((pairs, 2, order, order), jnp.float32),
+                pltpu.SemaphoreType.DMA((pairs,)),
+            ],
         ),
         out_shape=jax.ShapeDtypeStruct(right.shape, jnp.float32),
+        compiler_params=PARAMS,
         name="pair_products",
     )(first_slot, nodes, right)
 
@@ -274,6 +295,7 @@
         ),
         out_shape=jax.ShapeDtypeStruct((RES_COL, 2, order, width * parts), jnp.float32),
         input_output_aliases=aliases,
+        compiler_params=PARAMS,
         name="second_products",
     )(*operands)
 
@@ -315,6 +337,7 @@
 
 def solution(mesh):
     placed = (P(("cfg", "node"), None, None, "pair"), P(), P(), P(), P(), P())
+
     return jax.shard_map(
         per_device,
         mesh=mesh,

time: 282 us -> 267 us (0.947)
  Pallas kernels: 62.5 us -> 50.6 us
  other arithmetic: 3.48 us -> 0.11 us
    pallas_call x8 -> x10, Pallas kernels: 31.8 us -> 23.6 us  [the longest x4 12.9 us: pick_own(): pl.pallas_call(own_kernel, in_specs=[SMEM, VMEM, VMEM, ANY], out_specs=VM...]
    pallas_call x2, Pallas kernels: 11.5 us -> 8.39 us  [pair_products(): pl.pallas_call(pair_kernel, grid_spec=pltpu.PrefetchScalarGridSpec(num_sc...]
  transfers between devices with their start and end apart: 12 -> 12, of which waited for: 8 -> 9; matrix products, arithmetic and copies ran while one was open for 4% -> 2% of each run, Pallas kernels for 19% -> 16%
where the time goes in v3:
time: 267 us; the launch traced here: 266 us
  waiting for transfers between devices  156 us (58%)
  Pallas kernels  50.6 us (19%)
  starting transfers between devices  46.9 us (18%)
  local copies, waits for them, and re-layouts  10.9 us (4%)
    ppermute x4, waiting for transfers between devices, fetch_items(): recv = lax.ppermute(leaving, 'node', swap)  101 us
    all_to_all x4, waiting for transfers between devices, fetch_items(): lax.all_to_all(part, 'node', 0, 0, axis_index_groups=halves, tiled=True)  34.9 us
    all_to_all x4, starting transfers between devices, fetch_items(): lax.all_to_all(picked, 'node', 0, 0, axis_index_groups=halves, tiled=True)  22.2 us
    all_to_all x4, waiting for transfers between devices, fetch_items(): lax.all_to_all(picked, 'node', 0, 0, axis_index_groups=halves, tiled=True)  20.1 us
    all_to_all x4, starting transfers between devices, fetch_items(): lax.all_to_all(part, 'node', 0, 0, axis_index_groups=halves, tiled=True)  18.6 us
    pallas_call x4, Pallas kernels, pick_own(): pl.pallas_call(own_kernel, in_specs=[SMEM, VMEM, VMEM, ANY], out_specs=VM...  12.9 us
    pallas_call x2, Pallas kernels, second_products(): pl.pallas_call(functools.partial(second_kernel, len(lefts)), grid_spec=pl...  10.9 us
    pallas_call x2, Pallas kernels, pair_products(): pl.pallas_call(pair_kernel, grid_spec=pltpu.PrefetchScalarGridSpec(num_sc...  8.39 us
  transfers between devices with their start and end apart: 12, of which 9 were waited for; matrix products, arithmetic and copies ran while one was open for 2% of the time, Pallas kernels for 16%

profile of v3, /device:TPU:0, one launch (start us, length us, event | category | flops | bytes accessed | tf_op | source)
XLA Modules:
  0.0 265.8 jit_solution(8849753158789425243)
XLA Ops:
  0.0 3.8 %cut_rows.2 = f32[16,8,2,16,128]{4,3,2,1,0:T(8,128)} custom-call(f32[8,2,256,256]{3,2,1,0:T(8,128)} %nodes_ref.3), custom_call_target="tpu_custom_call" | custom-call | tf_op jit(solution)/shard_map/cut_rows/pallas_call | solution.py:31
  3.9 6.3 %all-to-all-start = ((f32[16,8,2,16,128]{4,3,2,1,0:T(8,128)}), f32[16,8,2,16,128]{4,3,2,1,0:T(8,128)S(1)}, u32[]{:S(2)}, u32[]{:S(2)}) async-start(f32[16,8,2,16,128]{4,3,2,1,0:T(8,128)} %cut_rows.2), calls=%async_computation | async-start | bytes 4194304 | tf_op jit(solution)/shard_map/all_to_all | solution.py:171
  10.2 3.9 %cut_rows.3 = f32[16,8,2,16,128]{4,3,2,1,0:T(8,128)} custom-call(f32[8,2,256,256]{3,2,1,0:T(8,128)} %nodes_ref.3), custom_call_target="tpu_custom_call" | custom-call | tf_op jit(solution)/shard_map/cut_rows/pallas_call | solution.py:31
  14.0 25.2 %all-to-all-done = f32[16,8,2,16,128]{4,3,2,1,0:T(8,128)S(1)} async-done(((f32[16,8,2,16,128]{4,3,2,1,0:T(8,128)}), f32[16,8,2,16,128]{4,3,2,1,0:T(8,128)S(1)}, u32[]{:S(2)}, u32[]{:S(2)}) %all-to-all-start) | async-done | bytes 2097184 | tf_op jit(solution)/shard_map/all_to_all | solution.py:171
  39.2 5.0 %all-to-all-start.2 = ((f32[16,8,2,16,128]{4,3,2,1,0:T(8,128)}), f32[16,8,2,16,128]{4,3,2,1,0:T(8,128)}, u32[]{:S(2)}, u32[]{:S(2)}) async-start(f32[16,8,2,16,128]{4,3,2,1,0:T(8,128)} %cut_rows.3), calls=%async_computation.2 | async-start | bytes 4194304 | tf_op jit(solution)/shard_map/all_to_all | solution.py:171
  45.5 3.9 %make_plan.2 = (s32[128]{0:T(128)S(1)}, s32[64]{0:T(128)S(1)}, s32[1]{0:T(128)}) custom-call(s32[1]{0:T(128)} %bitcast.2.half_ref, s32[128]{0:T(128)S(1)} %gather_fusion.1), custom_call_target="tpu_custom_call" | custom-call | tf_op jit(solution)/shard_map/make_plan/pallas_call | solution.py:88
  50.1 2.7 collective-permute-start.4
  54.7 29.1 %collective-permute-done.4.recv_ref = f32[36,2,16,128]{3,2,1,0:T(8,128)S(1)} collective-permute-done((f32[36,2,16,128]{3,2,1,0:T(8,128)S(1)}, f32[36,2,16,128]{3,2,1,0:T(8,128)S(1)}, u32[]{:S(2)}, u32[]{:S(2)}) %collective-permute-start.4) | collective-permute-done | bytes 589856 | tf_op jit(solution)/shard_map/ppermute | solution.py:174
  83.9 2.9 %pick_own.4 = f32[64,2,16,128]{3,2,1,0:T(8,128)} custom-call(s32[64]{0:T(128)S(1)} %get-tuple-element.47.source_ref, f32[128,2,16,128]{3,2,1,0:T(8,128)S(1)} %bitcast.21, f32[36,2,16,128]{3,2,1,0:T(8,128)S(1)} %collective-permute-done.4.recv_ref, f32[92,2,16,128]{3,2,1,0:T(8,128)} %get-tuple-element.53.extra_ref), custom_call_target="tpu_custom_call" | custom-call | tf_op jit(solution)/shard_map/pick_own/pallas_call | solution.py:148
  86.8 7.6 %all-to-all-start.1 = ((f32[16,4,2,16,128]{4,3,2,1,0:T(8,128)}), f32[16,4,2,16,128]{4,3,2,1,0:T(8,128)S(1)}, u32[]{:S(2)}, u32[]{:S(2)}) async-start(f32[16,4,2,16,128]{4,3,2,1,0:T(8,128)} %bitcast.6), calls=%async_computation.1 | async-start | bytes 2097152 | tf_op jit(solution)/shard_map/all_to_all | solution.py:184
  97.5 27.9 %collective-permute-done.5.recv_ref = f32[36,2,16,128]{3,2,1,0:T(8,128)S(1)} collective-permute-done((f32[36,2,16,128]{3,2,1,0:T(8,128)S(1)}, f32[36,2,16,128]{3,2,1,0:T(8,128)S(1)}, u32[]{:S(2)}, u32[]{:S(2)}) %collective-permute-start.5) | collective-permute-done | bytes 589856 | tf_op jit(solution)/shard_map/ppermute | solution.py:174
  125.4 4.0 %pick_own.5 = f32[64,2,16,128]{3,2,1,0:T(8,128)} custom-call(s32[64]{0:T(128)S(1)} %get-tuple-element.47.source_ref, f32[128,2,16,128]{3,2,1,0:T(8,128)} %bitcast.7.spread_ref, f32[36,2,16,128]{3,2,1,0:T(8,128)S(1)} %collective-permute-done.5.recv_ref, f32[92,2,16,128]{3,2,1,0:T(8,128)} %get-tuple-element.54.extra_ref), custom_call_target="tpu_custom_call" | custom-call | tf_op jit(solution)/shard_map/pick_own/pallas_call | solution.py:148
  129.4 3.9 %all-to-all-start.3 = ((f32[16,4,2,16,128]{4,3,2,1,0:T(8,128)}), f32[16,4,2,16,128]{4,3,2,1,0:T(8,128)S(1)}, u32[]{:S(2)}, u32[]{:S(2)}) async-start(f32[16,4,2,16,128]{4,3,2,1,0:T(8,128)} %bitcast.8), calls=%async_computation.3 | async-start | bytes 2097152 | tf_op jit(solution)/shard_map/all_to_all | solution.py:184
  134.1 2.2 copy-done.1
  136.3 4.2 %pair_products.2.refs_0_ = f32[16,4,2,16,128]{4,3,2,1,0:T(8,128)} custom-call(s32[4]{0:T(128)S(1)} %broadcast_subtract_fusion.first_ref, f32[8,2,256,256]{3,2,1,0:T(8,128)S(1)} %copy-done.1, f32[16,4,2,16,128]{4,3,2,1,0:T(8,128)S(1)} %all-to-all-done.1.right_ref), custom_call_target="tpu_custom_call" | custom-call | tf_op jit(solution)/shard_map/pair_products/pallas_call | solution.py:232
  140.5 9.0 %all-to-all-done.3.right_ref = f32[16,4,2,16,128]{4,3,2,1,0:T(8,128)S(1)} async-done(((f32[16,4,2,16,128]{4,3,2,1,0:T(8,128)}), f32[16,4,2,16,128]{4,3,2,1,0:T(8,128)S(1)}, u32[]{:S(2)}, u32[]{:S(2)}) %all-to-all-start.3) | async-done | bytes 1048608 | tf_op jit(solution)/shard_map/all_to_all | solution.py:184
  149.5 3.7 %all-to-all-start.6 = ((f32[16,4,2,16,128]{4,3,2,1,0:T(8,128)}), f32[16,4,2,16,128]{4,3,2,1,0:T(8,128)S(1)}, u32[]{:S(2)}, u32[]{:S(2)}) async-start(f32[16,4,2,16,128]{4,3,2,1,0:T(8,128)} %pair_products.2.refs_0_), calls=%async_computation.6 | async-start | bytes 2097152 | tf_op jit(solution)/shard_map/all_to_all | solution.py:171
  153.2 2.2 copy-done.2
  155.4 4.2 %pair_products.3.refs_1_ = f32[16,4,2,16,128]{4,3,2,1,0:T(8,128)} custom-call(s32[4]{0:T(128)S(1)} %broadcast_subtract_fusion.first_ref, f32[8,2,256,256]{3,2,1,0:T(8,128)S(1)} %copy-done.2, f32[16,4,2,16,128]{4,3,2,1,0:T(8,128)S(1)} %all-to-all-done.3.right_ref), custom_call_target="tpu_custom_call" | custom-call | tf_op jit(solution)/shard_map/pair_products/pallas_call | solution.py:232
  159.6 9.7 %all-to-all-done.6 = f32[16,4,2,16,128]{4,3,2,1,0:T(8,128)S(1)} async-done(((f32[16,4,2,16,128]{4,3,2,1,0:T(8,128)}), f32[16,4,2,16,128]{4,3,2,1,0:T(8,128)S(1)}, u32[]{:S(2)}, u32[]{:S(2)}) %all-to-all-start.6) | async-done | bytes 1048608 | tf_op jit(solution)/shard_map/all_to_all | solution.py:171
  169.3 3.7 %all-to-all-start.4 = ((f32[16,4,2,16,128]{4,3,2,1,0:T(8,128)}), f32[16,4,2,16,128]{4,3,2,1,0:T(8,128)S(1)}, u32[]{:S(2)}, u32[]{:S(2)}) async-start(f32[16,4,2,16,128]{4,3,2,1,0:T(8,128)} %pair_products.3.refs_1_), calls=%async_computation.4 | async-start | bytes 2097152 | tf_op jit(solution)/shard_map/all_to_all | solution.py:171
  173.0 3.3 %make_plan.3 = (s32[64]{0:T(128)S(1)}, s32[64]{0:T(128)S(1)}, s32[1]{0:T(128)}) custom-call(s32[1]{0:T(128)} %bitcast.2.half_ref, s32[128]{0:T(128)S(1)} %slice_bitcast_fusion.ids_ref), custom_call_target="tpu_custom_call" | custom-call | tf_op jit(solution)/shard_map/make_plan/pallas_call | solution.py:88
  179.7 23.6 %collective-permute-done.7.recv_ref = f32[32,2,16,128]{3,2,1,0:T(8,128)S(1)} collective-permute-done((f32[32,2,16,128]{3,2,1,0:T(8,128)S(1)}, f32[32,2,16,128]{3,2,1,0:T(8,128)S(1)}, u32[]{:S(2)}, u32[]{:S(2)}) %collective-permute-start.7) | collective-permute-done | bytes 524320 | tf_op jit(solution)/shard_map/ppermute | solution.py:174
  203.3 3.0 %pick_own.7 = f32[64,2,16,128]{3,2,1,0:T(8,128)} custom-call(s32[64]{0:T(128)S(1)} %get-tuple-element.50.source_ref, f32[64,2,16,128]{3,2,1,0:T(8,128)S(1)} %bitcast.27, f32[32,2,16,128]{3,2,1,0:T(8,128)S(1)} %collective-permute-done.7.recv_ref, f32[32,2,16,128]{3,2,1,0:T(8,128)} %get-tuple-element.56.extra_ref), custom_call_target="tpu_custom_call" | custom-call | tf_op jit(solution)/shard_map/pick_own/pallas_call | solution.py:148
  206.2 4.0 %all-to-all-start.7 = ((f32[16,4,2,16,128]{4,3,2,1,0:T(8,128)}), f32[16,4,2,16,128]{4,3,2,1,0:T(8,128)S(1)}, u32[]{:S(2)}, u32[]{:S(2)}) async-start(f32[16,4,2,16,128]{4,3,2,1,0:T(8,128)} %bitcast.14), calls=%async_computation.7 | async-start | bytes 2097152 | tf_op jit(solution)/shard_map/all_to_all | solution.py:184
  210.8 2.2 collective-permute-start.6
  213.9 20.1 %collective-permute-done.6.recv_ref = f32[32,2,16,128]{3,2,1,0:T(8,128)S(1)} collective-permute-done((f32[32,2,16,128]{3,2,1,0:T(8,128)S(1)}, f32[32,2,16,128]{3,2,1,0:T(8,128)S(1)}, u32[]{:S(2)}, u32[]{:S(2)}) %collective-permute-start.6) | collective-permute-done | bytes 524320 | tf_op jit(solution)/shard_map/ppermute | solution.py:174
  233.9 3.0 %pick_own.6 = f32[64,2,16,128]{3,2,1,0:T(8,128)} custom-call(s32[64]{0:T(128)S(1)} %get-tuple-element.50.source_ref, f32[64,2,16,128]{3,2,1,0:T(8,128)S(1)} %bitcast.24, f32[32,2,16,128]{3,2,1,0:T(8,128)S(1)} %collective-permute-done.6.recv_ref, f32[32,2,16,128]{3,2,1,0:T(8,128)} %get-tuple-element.55.extra_ref), custom_call_target="tpu_custom_call" | custom-call | tf_op jit(solution)/shard_map/pick_own/pallas_call | solution.py:148
  237.5 6.7 %all-to-all-start.5 = ((f32[16,4,2,16,128]{4,3,2,1,0:T(8,128)}), f32[16,4,2,16,128]{4,3,2,1,0:T(8,128)S(1)}, u32[]{:S(2)}, u32[]{:S(2)}) async-start(f32[16,4,2,16,128]{4,3,2,1,0:T(8,128)} %bitcast.12), calls=%async_computation.5 | async-start | bytes 2097152 | tf_op jit(solution)/shard_map/all_to_all | solution.py:184
  244.5 5.4 %second_products.2.refs_3_ = f32[2,2,256,256]{3,2,1,0:T(8,128)} custom-call(s32[4]{0:T(128)S(1)} %subtract_bitcast_fusion.left_index, s32[4]{0:T(128)S(1)} %dynamic-slice_subtract_fusion.target, s32[4]{0:T(128)S(1)} %dynamic_slice.14.sign, f32[16,4,2,16,128]{4,3,2,1,0:T(8,128)} %pair_products.2.refs_0_, f32[16,4,2,16,128]{4,3,2,1,0:T(8,128)} %pair_products.3.refs_1_, ...), custom_call_target="tpu_custom_call" | custom-call | tf_op jit(solution)/shard_map/second_products/pallas_call | solution.py:286
  249.9 10.5 %all-to-all-done.5.refs_2_ = f32[16,4,2,16,128]{4,3,2,1,0:T(8,128)S(1)} async-done(((f32[16,4,2,16,128]{4,3,2,1,0:T(8,128)}), f32[16,4,2,16,128]{4,3,2,1,0:T(8,128)S(1)}, u32[]{:S(2)}, u32[]{:S(2)}) %all-to-all-start.5) | async-done | bytes 1048608 | tf_op jit(solution)/shard_map/all_to_all | solution.py:184
  260.4 5.4 %second_products.3 = f32[2,2,256,256]{3,2,1,0:T(8,128)} custom-call(s32[4]{0:T(128)S(1)} %subtract_bitcast_fusion.left_index, s32[4]{0:T(128)S(1)} %dynamic-slice_subtract_fusion.target, s32[4]{0:T(128)S(1)} %dynamic_slice.14.sign, f32[16,4,2,16,128]{4,3,2,1,0:T(8,128)} %pair_products.2.refs_0_, ...), custom_call_target="tpu_custom_call", output_to_operand_aliasing={{}: (6, {})} | custom-call | tf_op jit(solution)/shard_map/second_products/pallas_call | solution.py:286
  (43 shorter events, 16.5 us)
Async XLA Ops:
  0.0 44.3 %copy-start = (s32[256]{0:T(256)S(1)}, s32[256]{0:T(256)}, u32[]{:S(2)}) copy-start(s32[256]{0:T(256)} %param.15) | copy-start | bytes 3076
  3.9 35.4 %all-to-all-start = ((f32[16,8,2,16,128]{4,3,2,1,0:T(8,128)}), f32[16,8,2,16,128]{4,3,2,1,0:T(8,128)S(1)}, u32[]{:S(2)}, u32[]{:S(2)}) async-start(f32[16,8,2,16,128]{4,3,2,1,0:T(8,128)} %cut_rows.2), calls=%async_computation | async-start | bytes 4194304 | tf_op jit(solution)/shard_map/all_to_all | solution.py:171
  14.0 30.2 %copy-start.3 = (s32[128,2]{0,1:T(2,128)S(1)}, s32[128,2]{0,1:T(2,128)}, u32[]{:S(2)}) copy-start(s32[128,2]{0,1:T(2,128)} %param.16) | copy-start | bytes 3076
  39.2 47.6 %all-to-all-start.2 = ((f32[16,8,2,16,128]{4,3,2,1,0:T(8,128)}), f32[16,8,2,16,128]{4,3,2,1,0:T(8,128)}, u32[]{:S(2)}, u32[]{:S(2)}) async-start(f32[16,8,2,16,128]{4,3,2,1,0:T(8,128)} %cut_rows.3), calls=%async_computation.2 | async-start | bytes 4194304 | tf_op jit(solution)/shard_map/all_to_all | solution.py:171
  50.1 33.8 %collective-permute-start.4 = (f32[36,2,16,128]{3,2,1,0:T(8,128)S(1)}, f32[36,2,16,128]{3,2,1,0:T(8,128)S(1)}, u32[]{:S(2)}, u32[]{:S(2)}) collective-permute-start(f32[36,2,16,128]{3,2,1,0:T(8,128)S(1)} %pick_cross.12), channel_id=1, source_target_pairs={{0,16},{1,17},{2,18},{3,19},{4,20},{5,21},{6,22},{7,23},{8,24},{9,... | collective-permute-start | bytes 1769480 | tf_op jit(solution)/shard_map/ppermute | solution.py:174
  86.8 42.6 %all-to-all-start.1 = ((f32[16,4,2,16,128]{4,3,2,1,0:T(8,128)}), f32[16,4,2,16,128]{4,3,2,1,0:T(8,128)S(1)}, u32[]{:S(2)}, u32[]{:S(2)}) async-start(f32[16,4,2,16,128]{4,3,2,1,0:T(8,128)} %bitcast.6), calls=%async_computation.1 | async-start | bytes 2097152 | tf_op jit(solution)/shard_map/all_to_all | solution.py:184
  96.1 29.3 %collective-permute-start.5 = (f32[36,2,16,128]{3,2,1,0:T(8,128)S(1)}, f32[36,2,16,128]{3,2,1,0:T(8,128)S(1)}, u32[]{:S(2)}, u32[]{:S(2)}) collective-permute-start(f32[36,2,16,128]{3,2,1,0:T(8,128)S(1)} %pick_cross.13), channel_id=1, source_target_pairs={{0,16},{1,17},{2,18},{3,19},{4,20},{5,21},{6,22},{7,23},{8,24},{9,... | collective-permute-start | bytes 1769480 | tf_op jit(solution)/shard_map/ppermute | solution.py:174
  129.4 20.1 %all-to-all-start.3 = ((f32[16,4,2,16,128]{4,3,2,1,0:T(8,128)}), f32[16,4,2,16,128]{4,3,2,1,0:T(8,128)S(1)}, u32[]{:S(2)}, u32[]{:S(2)}) async-start(f32[16,4,2,16,128]{4,3,2,1,0:T(8,128)} %bitcast.8), calls=%async_computation.3 | async-start | bytes 2097152 | tf_op jit(solution)/shard_map/all_to_all | solution.py:184
  134.1 2.2 copy-start.1
  149.5 19.8 %all-to-all-start.6 = ((f32[16,4,2,16,128]{4,3,2,1,0:T(8,128)}), f32[16,4,2,16,128]{4,3,2,1,0:T(8,128)S(1)}, u32[]{:S(2)}, u32[]{:S(2)}) async-start(f32[16,4,2,16,128]{4,3,2,1,0:T(8,128)} %pair_products.2.refs_0_), calls=%async_computation.6 | async-start | bytes 2097152 | tf_op jit(solution)/shard_map/all_to_all | solution.py:171
  153.2 2.2 copy-start.2
  159.6 13.4 %copy-start.4 = (s32[128,2]{0,1:T(2,128)S(1)}, s32[128,2]{0,1:T(2,128)}, u32[]{:S(2)}) copy-start(s32[128,2]{0,1:T(2,128)} %param.17) | copy-start | bytes 3076
  169.3 37.0 %all-to-all-start.4 = ((f32[16,4,2,16,128]{4,3,2,1,0:T(8,128)}), f32[16,4,2,16,128]{4,3,2,1,0:T(8,128)S(1)}, u32[]{:S(2)}, u32[]{:S(2)}) async-start(f32[16,4,2,16,128]{4,3,2,1,0:T(8,128)} %pair_products.3.refs_1_), calls=%async_computation.4 | async-start | bytes 2097152 | tf_op jit(solution)/shard_map/all_to_all | solution.py:171
  176.9 26.4 %collective-permute-start.7 = (f32[32,2,16,128]{3,2,1,0:T(8,128)S(1)}, f32[32,2,16,128]{3,2,1,0:T(8,128)S(1)}, u32[]{:S(2)}, u32[]{:S(2)}) collective-permute-start(f32[32,2,16,128]{3,2,1,0:T(8,128)S(1)} %pick_cross.15), channel_id=1, source_target_pairs={{0,16},{1,17},{2,18},{3,19},{4,20},{5,21},{6,22},{7,23},{8,24},{9,... | collective-permute-start | bytes 1572872 | tf_op jit(solution)/shard_map/ppermute | solution.py:174
  206.2 31.3 %all-to-all-start.7 = ((f32[16,4,2,16,128]{4,3,2,1,0:T(8,128)}), f32[16,4,2,16,128]{4,3,2,1,0:T(8,128)S(1)}, u32[]{:S(2)}, u32[]{:S(2)}) async-start(f32[16,4,2,16,128]{4,3,2,1,0:T(8,128)} %bitcast.14), calls=%async_computation.7 | async-start | bytes 2097152 | tf_op jit(solution)/shard_map/all_to_all | solution.py:184
  210.8 23.1 %collective-permute-start.6 = (f32[32,2,16,128]{3,2,1,0:T(8,128)S(1)}, f32[32,2,16,128]{3,2,1,0:T(8,128)S(1)}, u32[]{:S(2)}, u32[]{:S(2)}) collective-permute-start(f32[32,2,16,128]{3,2,1,0:T(8,128)S(1)} %pick_cross.14), channel_id=1, source_target_pairs={{0,16},{1,17},{2,18},{3,19},{4,20},{5,21},{6,22},{7,23},{8,24},{9,... | collective-permute-start | bytes 1572872 | tf_op jit(solution)/shard_map/ppermute | solution.py:174
  236.9 7.3 %copy-start.6 = (s32[128]{0:T(128)S(1)}, s32[128]{0:T(128)}, u32[]{:S(2)}) copy-start(s32[128]{0:T(128)} %param.19) | copy-start | bytes 1540
  236.9 7.4 %copy-start.5 = (s32[128]{0:T(128)S(1)}, s32[128]{0:T(128)}, u32[]{:S(2)}) copy-start(s32[128]{0:T(128)} %param.18) | copy-start | bytes 1540
  237.5 22.8 %all-to-all-start.5 = ((f32[16,4,2,16,128]{4,3,2,1,0:T(8,128)}), f32[16,4,2,16,128]{4,3,2,1,0:T(8,128)S(1)}, u32[]{:S(2)}, u32[]{:S(2)}) async-start(f32[16,4,2,16,128]{4,3,2,1,0:T(8,128)} %bitcast.12), calls=%async_computation.5 | async-start | bytes 2097152 | tf_op jit(solution)/shard_map/all_to_all | solution.py:184

commit v4 on v1

v4 whole, which is shorter than its diff:
```python
import functools

import jax
import jax.numpy as jnp
from jax import lax
from jax.experimental import pallas as pl
from jax.experimental.pallas import tpu as pltpu
from jax.sharding import PartitionSpec as P


RES_COL = 2
LANES = 128
EARLY_SHARE = 27 / 64
LATE_SHARE = 3 / 32
ANY = pl.BlockSpec(memory_space=pl.ANY)
HBM = pl.BlockSpec(memory_space=pltpu.HBM)
SMEM = pl.BlockSpec(memory_space=pltpu.SMEM)
VMEM = pl.BlockSpec(memory_space=pltpu.VMEM)
PARAMS = pltpu.CompilerParams(vmem_limit_bytes=24 * 1024 * 1024)


def cut_kernel(in_ref, out_ref):
    rows = out_ref.shape[3]
    for j in range(out_ref.shape[0]):
        out_ref[j] = in_ref[:, :, j * rows : (j + 1) * rows, :]


def cut_rows(nodes, group, part, width):
    count, _, order, _ = nodes.shape
    rows = order // group
    steps = 4 if group % 4 == 0 else 1
    return pl.pallas_call(
        cut_kernel,
        grid=(steps,),
        in_specs=[pl.BlockSpec((count, 2, order // steps, width), lambda i: (0, 0, i, part))],
        out_specs=pl.BlockSpec((group // steps, count, 2, rows, width), lambda i: (i, 0, 0, 0, 0)),
        out_shape=jax.ShapeDtypeStruct((group, count, 2, rows, width), jnp.float32),
        name="cut_rows",
    )(nodes)


def plan_kernel(rooms, half_ref, *refs):
    ids_refs, send_refs, source_refs = refs[:2], refs[2:4], refs[4:6]
    crowded_ref, place_ref = refs[6:]
    half = half_ref[0]
    count = send_refs[0].shape[0]
    bases = (count, count + rooms[0])
    everything = count + rooms[0] + rooms[1]

    def clear(i, carry):
        place_ref[i] = -1
        return carry

    def empty(i, carry):
        for send_ref in send_refs:
            send_ref[i] = 0
        return carry

    lax.fori_loop(0, 2 * count, clear, 0, unroll=8)
    lax.fori_loop(0, count, empty, 0, unroll=8)
    most = jnp.int32(0)
    for ids_ref, send_ref, source_ref, base, room in zip(
        ids_refs, send_refs, source_refs, bases, rooms
    ):
        asked = source_ref.shape[0]

        def visit_other(q, found):
            item = ids_ref[(1 - half) * asked + q]
            here = item - half * count
            fresh = (here >= 0) & (here < count) & (place_ref[item] < 0)

            @pl.when(fresh)
            def _():
                place_ref[item] = 0
                send_ref[found] = here

            return found + fresh.astype(jnp.int32)

        def visit_own(q, found):
            item = ids_ref[half * asked + q]
            here = item - half * count
            inside = (here >= 0) & (here < count)
            known = place_ref[item]
            fresh = jnp.logical_not(inside) & (known < 0)
            there = everything + item - (1 - half) * count
            place = jnp.where(known < 0, jnp.where(found < room, base + found, there), known)

            @pl.when(fresh)
            def _():
                place_ref[item] = place

            source_ref[q] = jnp.where(inside, here, place)
            return found + fresh.astype(jnp.int32)

        sent = lax.fori_loop(0, asked, visit_other, jnp.int32(0))
        received = lax.fori_loop(0, asked, visit_own, jnp.int32(0))
        most = jnp.maximum(most, jnp.maximum(sent, received) - room)
    crowded_ref[0] = (most > 0).astype(jnp.int32)


def make_plan(half, early, late, count, rooms):
    whole = jax.ShapeDtypeStruct((count,), jnp.int32)
    return pl.pallas_call(
        functools.partial(plan_kernel, rooms),
        in_specs=[SMEM] * 3,
        out_specs=[SMEM] * 5,
        out_shape=[
            whole,
            whole,
            jax.ShapeDtypeStruct((early.shape[0] // 2,), jnp.int32),
            jax.ShapeDtypeStruct((late.shape[0] // 2,), jnp.int32),
            jax.ShapeDtypeStruct((1,), jnp.int32),
        ],
        scratch_shapes=[pltpu.SMEM((2 * count,), jnp.int32)],
        compiler_params=PARAMS,
        name="make_plan",
    )(half, early, late)


def leave_kernel(send_ref, *refs):
    spread_refs, out_ref = refs[:-1], refs[-1]
    for c, spread_ref in enumerate(spread_refs):

        def copy(i, carry):
            out_ref[i, c] = spread_ref[send_ref[i]]
            return carry

        lax.fori_loop(0, out_ref.shape[0], copy, 0, unroll=4)


def pick_leaving(send, spreads, room):
    return pl.pallas_call(
        leave_kernel,
        in_specs=[SMEM] + [VMEM] * len(spreads),
        out_specs=VMEM,
        out_shape=jax.ShapeDtypeStruct((room, len(spreads)) + spreads[0].shape[1:], jnp.float32),
        compiler_params=PARAMS,
        name="pick_leaving",
    )(send, *spreads)


def collect_kernel(parts, bounds, source_ref, *refs):
    spread_refs, early_refs, extra_refs = (refs[i * parts : (i + 1) * parts] for i in range(3))
    late_ref = refs[3 * parts] if bounds[2] > bounds[1] else None
    out_ref, sem = refs[-2:]
    here, early, late = bounds

    def copy(q, carry):
        source = source_ref[q]

        @pl.when(source < here)
        def _():
            for c in range(parts):
                out_ref[q, c] = spread_refs[c][source]

        @pl.when((source >= here) & (source < early))
        def _():
            for c in range(parts):
                out_ref[q, c] = early_refs[c][source - here, 0]

        if late_ref is not None:

            @pl.when((source >= early) & (source < late))
            def _():
                for c in range(parts):
                    out_ref[q, c] = late_ref[source - early, c]

        return carry

    lax.fori_loop(0, out_ref.shape[0], copy, 0)

    def fetch(q, carry):
        source = source_ref[q] - late

        @pl.when(source >= 0)
        def _():
            for c in range(parts):
                slow = pltpu.make_async_copy(extra_refs[c].at[source], out_ref.at[q, c], sem)
                slow.start()
                slow.wait()

        return carry

    lax.fori_loop(0, out_ref.shape[0], fetch, 0)


def collect(source, spreads, earlies, extras, late, bounds):
    parts = len(spreads)
    arrays = [*spreads, *earlies, *extras]
    specs = [VMEM] * (2 * parts) + [ANY] * parts
    if late is not None:
        arrays.append(late)
        specs.append(VMEM)
    return pl.pallas_call(
        functools.partial(collect_kernel, parts, bounds),
        in_specs=[SMEM] + specs,
        out_specs=VMEM,
        out_shape=jax.ShapeDtypeStruct(
            (source.shape[0], parts) + spreads[0].shape[1:], jnp.float32
        ),
        scratch_shapes=[pltpu.SemaphoreType.DMA],
        compiler_params=PARAMS,
        name="collect",
    )(source, *arrays)


def fetch_items(cuts, early_ids, late_ids):
    devices = lax.axis_size("node")
    group = devices // 2
    half = (lax.axis_index("node") // group).astype(jnp.int32).reshape(1)
    halves = [[h * group + i for i in range(group)] for h in range(2)]
    swap = [(i, (i + group) % devices) for i in range(devices)]
    count = group * cuts[0].shape[1]
    rooms = tuple(min(count, max(8, int(count * share))) for share in (EARLY_SHARE, LATE_SHARE))
    send_early, send_late, early_source, late_source, crowded = make_plan(
        half, early_ids.reshape(-1), late_ids.reshape(-1), count, rooms
    )

    def exchange(x):
        x = x.reshape((group, x.shape[0] // group) + x.shape[1:])
        return lax.all_to_all(x, "node", 0, 0, axis_index_groups=halves, tiled=True)

    spreads, earlies, extras = [], [], []
    for cut in cuts:
        spread = lax.all_to_all(cut, "node", 0, 0, axis_index_groups=halves, tiled=True)
        spread = spread.reshape((count,) + spread.shape[2:])
        leaving = pick_leaving(send_early, [spread], rooms[0])
        earlies.append(lax.ppermute(leaving, "node", swap))
        extras.append(
            lax.cond(
                crowded[0] > 0,
                lambda x: lax.ppermute(x, "node", swap),
                jnp.zeros_like,
                spread,
            )
        )
        spreads.append(spread)
    leaving = pick_leaving(send_late, spreads, rooms[1])
    late = lax.ppermute(leaving, "node", swap)
    bounds = (count, count + rooms[0], count + rooms[0] + rooms[1])
    delivered = []
    for c in range(len(cuts)):
        picked = collect(
            early_source,
            spreads[c : c + 1],
            earlies[c : c + 1],
            extras[c : c + 1],
            None,
            (count, count + rooms[0], count + rooms[0]),
        )
        delivered.append(exchange(picked))
    picked = collect(late_source, spreads, earlies, extras, late, bounds)
    last = exchange(picked)
    return delivered, last


def product(left_real, left_imag, blocks):
    order = left_real.shape[1]
    right_real, right_imag = (
        jnp.concatenate([b[:, c].reshape(order, b.shape[-1]) for b in blocks], axis=1)
        for c in range(2)
    )
    stacked_left = jnp.concatenate([left_real, left_imag], axis=1)
    stacked_right = jnp.concatenate(
        [
            jnp.concatenate([right_real, right_imag], axis=1),
            jnp.concatenate([-right_imag, right_real], axis=1),
        ],
        axis=0,
    )
    return jnp.dot(
        stacked_left,
        stacked_right,
        precision=lax.Precision.HIGHEST,
        preferred_element_type=jnp.float32,
    )


def multiply_kernel(first_ref, left_ref, *refs):
    right_refs, out_ref, hold_ref, sems = refs[:-3], refs[-3], refs[-2], refs[-1]
    step = pl.program_id(0)
    width = out_ref.shape[-1]

    def fetch(k):
        return pltpu.make_async_copy(left_ref.at[first_ref[k]], hold_ref.at[k], sems.at[k])

    @pl.when(step == 0)
    def _():
        for k in range(hold_ref.shape[0]):
            fetch(k).start()

    fetch(step).wait()
    left = hold_ref[step]
    both = product(left[0], left[1], [ref[:, 0, 0] for ref in right_refs])
    out_ref[0, 0] = both[:, :width]
    out_ref[0, 1] = both[:, width:]


def multiply(left_index, lefts, rights, offset, number):
    group, _, _, _, rows, width = rights[0].shape
    order = lefts.shape[2]
    cols = width * len(rights)
    right_spec = pl.BlockSpec(
        (group, 1, 1, 2, rows, width), lambda k, index: (0, offset + k, 0, 0, 0, 0)
    )
    return pl.pallas_call(
        multiply_kernel,
        grid_spec=pltpu.PrefetchScalarGridSpec(
            num_scalar_prefetch=1,
            grid=(number,),
            in_specs=[HBM] + [right_spec] * len(rights),
            out_specs=pl.BlockSpec((1, 2, order, cols), lambda k, index: (k, 0, 0, 0)),
            scratch_shapes=[
                pltpu.VMEM((number, 2, order, order), jnp.float32),
                pltpu.SemaphoreType.DMA((number,)),
            ],
        ),
        out_shape=jax.ShapeDtypeStruct((number, 2, order, cols), jnp.float32),
        compiler_params=PARAMS,
        name="multiply",
    )(left_index, lefts, *rights)


def finish_kernel(target, sign, left_ref, right_ref, out_ref):
    step = pl.program_id(0)
    width = out_ref.shape[-1]

    @pl.when(step == 0)
    def _():
        out_ref[...] = jnp.zeros_like(out_ref)

    blocks = [right_ref[:, 0, c] for c in range(right_ref.shape[2])]
    both = product(left_ref[0, 0], left_ref[0, 1], blocks) * sign[step].astype(jnp.float32)
    row = target[step]
    out_ref[row, 0] += both[:, :width]
    out_ref[row, 1] += both[:, width:]


def finish(target, sign, lefts, right):
    group, seconds, parts, _, rows, width = right.shape
    order = lefts.shape[2]
    whole = (RES_COL, 2, order, width * parts)
    return pl.pallas_call(
        finish_kernel,
        grid_spec=pltpu.PrefetchScalarGridSpec(
            num_scalar_prefetch=2,
            grid=(seconds,),
            in_specs=[
                pl.BlockSpec((1, 2, order, order), lambda k, t, s: (k, 0, 0, 0)),
                pl.BlockSpec((group, 1, parts, 2, rows, width), lambda k, t, s: (0, k, 0, 0, 0, 0)),
            ],
            out_specs=pl.BlockSpec(whole, lambda k, t, s: (0, 0, 0, 0)),
        ),
        out_shape=jax.ShapeDtypeStruct(whole, jnp.float32),
        compiler_params=PARAMS,
        name="finish",
    )(target, sign, lefts, right)


def all_columns(x):
    if lax.axis_size("pair") == 1:
        return x
    return lax.all_gather(x, "pair", axis=3, tiled=True)


def per_device(node_blocks, node_slot, pair_list, second_list, targets, spin_signs):
    devices = lax.axis_size("node")
    column = lax.axis_index("node")
    group = devices // 2
    node_col, _, _, local_width = node_blocks.shape
    pair_col = pair_list.shape[0] // devices
    second_col = second_list.shape[0] // devices
    width = min(LANES, local_width)
    cuts = [cut_rows(node_blocks, group, c, width) for c in range(local_width // width)]

    slots = node_slot[pair_list]
    second_slots = slots[second_list[:, 1]]
    early_ids = jnp.concatenate(
        [slots[:, 1].reshape(devices, pair_col), second_slots[:, 0].reshape(devices, second_col)],
        axis=1,
    )
    late_ids = second_slots[:, 1].reshape(devices, second_col)
    rights, lasts = fetch_items(cuts, early_ids, late_ids)

    own_slots = lax.dynamic_slice_in_dim(slots, column * pair_col, pair_col, 0)
    first_slot = own_slots[:, 0] - column * node_col
    own_seconds = lax.dynamic_slice_in_dim(second_list, column * second_col, second_col, 0)
    left_index = own_seconds[:, 0] - column * pair_col
    own_signs = lax.dynamic_slice_in_dim(spin_signs, column * second_col, second_col, 0)
    own_targets = lax.dynamic_slice_in_dim(targets, column * second_col, second_col, 0)
    own_targets = own_targets - column * RES_COL

    products = multiply(first_slot, all_columns(node_blocks), rights, 0, pair_col)
    longer = multiply(left_index, all_columns(products), rights, pair_col, second_col)
    return finish(own_targets, own_signs, all_columns(longer), lasts)


def solution(mesh):
    placed = (P(("cfg", "node"), None, None, "pair"), P(), P(), P(), P(), P())

    return jax.shard_map(
        per_device,
        mesh=mesh,
        in_specs=placed,
        out_specs=P(("cfg", "node"), None, None, "pair"),
        check_vma=False,
    )
```

time: 309 us -> 255 us (0.83)
  waiting for transfers between devices: 226 us -> 147 us
  Pallas kernels: 0 us -> 55.3 us
  local copies, waits for them, and re-layouts: 43.7 us -> 16.2 us
  starting transfers between devices: 20.3 us -> 34.5 us
  matrix products: 10.7 us -> 0 us
  other arithmetic: 7.45 us -> 0.29 us
    all_to_all x4 -> x5, waiting for transfers between devices: 226 us -> 38.4 us  [the longest x2 25.2 us: fetch_items(): lax.all_to_all(cut, 'node', 0, 0, axis_index_groups=halves, tiled=True)]
    ppermute x0 -> x3, waiting for transfers between devices: none -> 108 us  [the longest x2 75.4 us: fetch_items(): earlies.append(lax.ppermute(leaving, 'node', swap))]
    pallas_call x0 -> x12, Pallas kernels: none -> 55.3 us  [the longest x3 15.5 us: collect(): pl.pallas_call(functools.partial(collect_kernel, parts, bounds), in_specs...]
    all_to_all x5 -> x0, local copies, waits for them, and re-layouts: 13.8 us -> none  [the longest x3 11.8 us: fetch_items(): lax.all_to_all(local_items, 'node', split_axis=2, concat_axis=0, tiled=True)]
    gather x6 -> x3, local copies, waits for them, and re-layouts: 14.8 us -> 2.73 us  [the longest x2 2.08 us: per_device(): slots = node_slot[pair_list]]
    dot_general x3 -> x0, matrix products: 10.7 us -> none  [the longest x2 7.48 us: complex_product(): jnp.einsum('jmk,jkn->jmn', stacked_left, stacked_right, precision=lax.Pre...]
    all_to_all x4 -> x5, starting transfers between devices: 20.3 us -> 28.4 us  [the longest x3 17.1 us: exchange(): return lax.all_to_all(x, 'node', 0, 0, axis_index_groups=halves, tiled=True)]
    select_n x9 -> x2, other arithmetic: 6.77 us -> 0.01 us  [the longest x1 0.01 us: per_device(): second_slots = slots[second_list[:, 1]]]
  transfers between devices with their start and end apart: 4 -> 8, of which waited for: 4 -> 5; matrix products, arithmetic and copies ran while one was open for 4% -> 3% of each run, Pallas kernels for 0% -> 18%
where the time goes in v4:
time: 255 us; the launch traced here: 254 us
  waiting for transfers between devices  147 us (58%)
  Pallas kernels  55.3 us (22%)
  starting transfers between devices  34.5 us (14%)
  local copies, waits for them, and re-layouts  16.2 us (6%)
    ppermute x2, waiting for transfers between devices, fetch_items(): earlies.append(lax.ppermute(leaving, 'node', swap))  75.4 us
    ppermute x1, waiting for transfers between devices, fetch_items(): late = lax.ppermute(leaving, 'node', swap)  32.9 us
    all_to_all x2, waiting for transfers between devices, fetch_items(): lax.all_to_all(cut, 'node', 0, 0, axis_index_groups=halves, tiled=True)  25.2 us
    all_to_all x3, starting transfers between devices, exchange(): return lax.all_to_all(x, 'node', 0, 0, axis_index_groups=halves, tiled=True)  17.1 us
    pallas_call x3, Pallas kernels, collect(): pl.pallas_call(functools.partial(collect_kernel, parts, bounds), in_specs...  15.5 us
    all_to_all x3, waiting for transfers between devices, exchange(): return lax.all_to_all(x, 'node', 0, 0, axis_index_groups=halves, tiled=True)  13.3 us
    pallas_call x2, Pallas kernels, multiply(): pl.pallas_call(multiply_kernel, grid_spec=pltpu.PrefetchScalarGridSpec(nu...  11.9 us
    all_to_all x2, starting transfers between devices, fetch_items(): lax.all_to_all(cut, 'node', 0, 0, axis_index_groups=halves, tiled=True)  11.3 us
  transfers between devices with their start and end apart: 8, of which 5 were waited for; matrix products, arithmetic and copies ran while one was open for 3% of the time, Pallas kernels for 18%

profile of v4, /device:TPU:0, one launch (start us, length us, event | category | flops | bytes accessed | tf_op | source)
XLA Modules:
  0.0 254.1 jit_solution(472838798273446720)
XLA Ops:
  0.0 3.9 %cut_rows.3 = f32[16,8,2,16,128]{4,3,2,1,0:T(8,128)} custom-call(f32[8,2,256,256]{3,2,1,0:T(8,128)} %left_ref.1), custom_call_target="tpu_custom_call" | custom-call | tf_op jit(solution)/shard_map/cut_rows/pallas_call | solution.py:32
  3.9 6.3 %all-to-all-start.2 = ((f32[16,8,2,16,128]{4,3,2,1,0:T(8,128)}), f32[16,8,2,16,128]{4,3,2,1,0:T(8,128)S(1)}, u32[]{:S(2)}, u32[]{:S(2)}) async-start(f32[16,8,2,16,128]{4,3,2,1,0:T(8,128)} %cut_rows.3), calls=%async_computation.2 | async-start | bytes 4194304 | tf_op jit(solution)/shard_map/all_to_all | solution.py:225
  10.2 3.9 %cut_rows.2 = f32[16,8,2,16,128]{4,3,2,1,0:T(8,128)} custom-call(f32[8,2,256,256]{3,2,1,0:T(8,128)} %left_ref.1), custom_call_target="tpu_custom_call" | custom-call | tf_op jit(solution)/shard_map/cut_rows/pallas_call | solution.py:32
  14.0 25.2 %all-to-all-done.2 = f32[16,8,2,16,128]{4,3,2,1,0:T(8,128)S(1)} async-done(((f32[16,8,2,16,128]{4,3,2,1,0:T(8,128)}), f32[16,8,2,16,128]{4,3,2,1,0:T(8,128)S(1)}, u32[]{:S(2)}, u32[]{:S(2)}) %all-to-all-start.2) | async-done | bytes 2097184 | tf_op jit(solution)/shard_map/all_to_all | solution.py:225
  39.2 5.0 %all-to-all-start = ((f32[16,8,2,16,128]{4,3,2,1,0:T(8,128)}), f32[16,8,2,16,128]{4,3,2,1,0:T(8,128)}, u32[]{:S(2)}, u32[]{:S(2)}) async-start(f32[16,8,2,16,128]{4,3,2,1,0:T(8,128)} %cut_rows.2), calls=%async_computation | async-start | bytes 4194304 | tf_op jit(solution)/shard_map/all_to_all | solution.py:225
  44.5 1.9 gather_fusion
  48.1 6.4 %make_plan.1 = (s32[128]{0:T(128)S(1)}, s32[128]{0:T(128)S(1)}, s32[128]{0:T(128)S(1)}, s32[64]{0:T(128)S(1)}, s32[1]{0:T(128)}) custom-call(s32[1]{0:T(128)} %bitcast.1.half_ref, s32[256]{0:T(256)S(1)} %reshape.36.refs_0_, s32[128]{0:T(128)S(1)} %get-tuple-element.23.refs_1_), custom_call_target="tpu_custom_call" | custom-call | tf_op jit(solution)/shard_map/make_plan/pallas_call | solution.py:103
  54.5 1.7 pick_leaving.4
  56.2 2.7 %collective-permute-start.3 = (f32[54,1,2,16,128]{4,3,2,1,0:T(8,128)S(1)}, f32[54,1,2,16,128]{4,3,2,1,0:T(8,128)S(1)}, u32[]{:S(2)}, u32[]{:S(2)}) collective-permute-start(f32[54,1,2,16,128]{4,3,2,1,0:T(8,128)S(1)} %pick_leaving.4), channel_id=1, source_target_pairs={{0,16},{1,17},{2,18},{3,19},{4,20},{5,21},{6,22},{7,23},{8,24},{9,... | collective-permute-start | bytes 2654216 | tf_op jit(solution)/shard_map/ppermute | solution.py:228
  59.5 1.6 conditional.3
  59.6 1.6 broadcast.12
  61.2 36.9 %collective-permute-done.3.refs_1_.refs_3_ = f32[54,1,2,16,128]{4,3,2,1,0:T(8,128)S(1)} collective-permute-done((f32[54,1,2,16,128]{4,3,2,1,0:T(8,128)S(1)}, f32[54,1,2,16,128]{4,3,2,1,0:T(8,128)S(1)}, u32[]{:S(2)}, u32[]{:S(2)}) %collective-permute-start.3) | collective-permute-done | bytes 884768 | tf_op jit(solution)/shard_map/ppermute | solution.py:228
  98.1 5.5 %collect.4 = f32[128,1,2,16,128]{4,3,2,1,0:T(8,128)S(1)} custom-call(s32[128]{0:T(128)S(1)} %get-tuple-element.18.source_ref, f32[128,2,16,128]{3,2,1,0:T(8,128)} %bitcast.16, f32[54,1,2,16,128]{4,3,2,1,0:T(8,128)S(1)} %collective-permute-done.3.refs_1_.refs_3_, f32[128,2,16,128]{3,2,1,0:T(8,128)} %get-tuple-element.26.refs_2_.refs_5_), custom_call_target="tpu_custom_call" | custom-call | tf_op jit(solution)/shard_map/collect/pallas_call | solution.py:194
  104.9 4.0 %all-to-all-start.3 = ((f32[16,8,1,2,16,128]{5,4,3,2,1,0:T(8,128)}), f32[16,8,1,2,16,128]{5,4,3,2,1,0:T(8,128)S(1)}, u32[]{:S(2)}, u32[]{:S(2)}) async-start(f32[16,8,1,2,16,128]{5,4,3,2,1,0:T(8,128)} %bitcast.12), calls=%async_computation.3 | async-start | bytes 4194304 | tf_op jit(solution)/shard_map/all_to_all | solution.py:221
  109.0 2.7 %pick_leaving.3 = f32[54,1,2,16,128]{4,3,2,1,0:T(8,128)} custom-call(s32[128]{0:T(128)S(1)} %get-tuple-element.19.send_ref, f32[128,2,16,128]{3,2,1,0:T(8,128)} %bitcast.3.refs_0_), custom_call_target="tpu_custom_call" | custom-call | tf_op jit(solution)/shard_map/pick_leaving/pallas_call | solution.py:132
  111.6 3.4 %collective-permute-start.2 = (f32[54,1,2,16,128]{4,3,2,1,0:T(8,128)}, f32[54,1,2,16,128]{4,3,2,1,0:T(8,128)}, u32[]{:S(2)}, u32[]{:S(2)}) collective-permute-start(f32[54,1,2,16,128]{4,3,2,1,0:T(8,128)} %pick_leaving.3), channel_id=1, source_target_pairs={{0,16},{1,17},{2,18},{3,19},{4,20},{5,21},{6,22},{7,23},{8,24},{9,... | collective-permute-start | bytes 2654216 | tf_op jit(solution)/shard_map/ppermute | solution.py:228
  115.0 1.6 conditional.2
  115.0 1.6 broadcast.11
  116.6 38.5 %collective-permute-done.2.refs_1_.refs_2_ = f32[54,1,2,16,128]{4,3,2,1,0:T(8,128)} collective-permute-done((f32[54,1,2,16,128]{4,3,2,1,0:T(8,128)}, f32[54,1,2,16,128]{4,3,2,1,0:T(8,128)}, u32[]{:S(2)}, u32[]{:S(2)}) %collective-permute-start.2) | collective-permute-done | bytes 884768 | tf_op jit(solution)/shard_map/ppermute | solution.py:228
  155.1 5.7 %collect.3 = f32[128,1,2,16,128]{4,3,2,1,0:T(8,128)S(1)} custom-call(s32[128]{0:T(128)S(1)} %get-tuple-element.18.source_ref, f32[128,2,16,128]{3,2,1,0:T(8,128)} %bitcast.3.refs_0_, f32[54,1,2,16,128]{4,3,2,1,0:T(8,128)} %collective-permute-done.2.refs_1_.refs_2_, f32[128,2,16,128]{3,2,1,0:T(8,128)} %get-tuple-element.25.refs_2_.refs_4_), custom_call_target="tpu_custom_call" | custom-call | tf_op jit(solution)/shard_map/collect/pallas_call | solution.py:194
  160.9 1.4 copy-done.4
  162.3 8.4 %all-to-all-start.1 = ((f32[16,8,1,2,16,128]{5,4,3,2,1,0:T(8,128)}), f32[16,8,1,2,16,128]{5,4,3,2,1,0:T(8,128)}, u32[]{:S(2)}, u32[]{:S(2)}) async-start(f32[16,8,1,2,16,128]{5,4,3,2,1,0:T(8,128)} %bitcast.13), calls=%async_computation.1 | async-start | bytes 4194304 | tf_op jit(solution)/shard_map/all_to_all | solution.py:221
  170.7 2.4 pick_leaving.5
  173.3 32.9 %collective-permute-done.4.refs_6_ = f32[12,2,2,16,128]{4,3,2,1,0:T(8,128)S(1)} collective-permute-done((f32[12,2,2,16,128]{4,3,2,1,0:T(8,128)S(1)}, f32[12,2,2,16,128]{4,3,2,1,0:T(8,128)S(1)}, u32[]{:S(2)}, u32[]{:S(2)}) %collective-permute-start.4) | collective-permute-done | bytes 393248 | tf_op jit(solution)/shard_map/ppermute | solution.py:239
  206.2 4.3 %collect.5 = f32[64,2,2,16,128]{4,3,2,1,0:T(8,128)S(1)} custom-call(s32[64]{0:T(128)S(1)} %get-tuple-element.21.source_ref, f32[128,2,16,128]{3,2,1,0:T(8,128)} %bitcast.3.refs_0_, f32[128,2,16,128]{3,2,1,0:T(8,128)S(1)} %bitcast.18, f32[54,1,2,16,128]{4,3,2,1,0:T(8,128)} %collective-permute-done.2.refs_1_.refs_2_, ...), custom_call_target="tpu_custom_call" | custom-call | tf_op jit(solution)/shard_map/collect/pallas_call | solution.py:194
  211.8 4.7 %all-to-all-start.4 = ((f32[16,4,2,2,16,128]{5,4,3,2,1,0:T(8,128)}), f32[16,4,2,2,16,128]{5,4,3,2,1,0:T(8,128)}, u32[]{:S(2)}, u32[]{:S(2)}) async-start(f32[16,4,2,2,16,128]{5,4,3,2,1,0:T(8,128)} %bitcast.11), calls=%async_computation.4 | async-start | bytes 4194304 | tf_op jit(solution)/shard_map/all_to_all | solution.py:221
  216.9 2.2 copy-done.1
  219.1 6.0 %multiply.2.left_ref = f32[4,2,256,256]{3,2,1,0:T(8,128)S(1)} custom-call(s32[4]{0:T(128)S(1)} %subtract_reduce_fusion.first_ref, f32[8,2,256,256]{3,2,1,0:T(8,128)S(1)} %copy-done.1, f32[16,8,1,2,16,128]{5,4,3,2,1,0:T(8,128)} %all-to-all-done.1.refs_0_, f32[16,8,1,2,16,128]{5,4,3,2,1,0:T(8,128)S(1)} %all-to-all-done.3.refs_1_), custom_call_target="tpu_custom_call" | custom-call | tf_op jit(solution)/shard_map/multiply/pallas_call | solution.py:306
  225.1 6.0 %multiply.3.left_ref = f32[4,2,256,256]{3,2,1,0:T(8,128)S(1)} custom-call(s32[4]{0:T(128)S(1)} %subtract_bitcast_fusion.first_ref, f32[4,2,256,256]{3,2,1,0:T(8,128)S(1)} %multiply.2.left_ref, f32[16,8,1,2,16,128]{5,4,3,2,1,0:T(8,128)} %all-to-all-done.1.refs_0_, f32[16,8,1,2,16,128]{5,4,3,2,1,0:T(8,128)S(1)} %all-to-all-done.3.refs_1_), custom_call_target="tpu_custom_call" | custom-call | tf_op jit(solution)/shard_map/multiply/pallas_call | solution.py:306
  232.4 13.2 %all-to-all-done.4.right_ref = f32[16,4,2,2,16,128]{5,4,3,2,1,0:T(8,128)} async-done(((f32[16,4,2,2,16,128]{5,4,3,2,1,0:T(8,128)}), f32[16,4,2,2,16,128]{5,4,3,2,1,0:T(8,128)}, u32[]{:S(2)}, u32[]{:S(2)}) %all-to-all-start.4) | async-done | bytes 2097184 | tf_op jit(solution)/shard_map/all_to_all | solution.py:221
  245.6 1.6 copy-done.6
  247.2 6.9 %finish.1 = f32[2,2,256,256]{3,2,1,0:T(8,128)} custom-call(s32[4]{0:T(128)S(1)} %dynamic-slice_subtract_fusion.target, s32[4]{0:T(128)S(1)} %dynamic_slice.13.sign, f32[4,2,256,256]{3,2,1,0:T(8,128)S(1)} %copy-done.6, f32[16,4,2,2,16,128]{5,4,3,2,1,0:T(8,128)} %all-to-all-done.4.right_ref), custom_call_target="tpu_custom_call" | custom-call | tf_op jit(solution)/shard_map/finish/pallas_call | solution.py:343
  (47 shorter events, 6.2 us)
Async XLA Ops:
  0.0 44.5 %copy-start = (s32[256]{0:T(256)S(1)}, s32[256]{0:T(256)}, u32[]{:S(2)}) copy-start(s32[256]{0:T(256)} %param.11) | copy-start | bytes 3076
  3.9 35.4 %all-to-all-start.2 = ((f32[16,8,2,16,128]{4,3,2,1,0:T(8,128)}), f32[16,8,2,16,128]{4,3,2,1,0:T(8,128)S(1)}, u32[]{:S(2)}, u32[]{:S(2)}) async-start(f32[16,8,2,16,128]{4,3,2,1,0:T(8,128)} %cut_rows.3), calls=%async_computation.2 | async-start | bytes 4194304 | tf_op jit(solution)/shard_map/all_to_all | solution.py:225
  14.0 30.2 %copy-start.9 = (s32[128,2]{0,1:T(2,128)S(1)}, s32[128,2]{0,1:T(2,128)}, u32[]{:S(2)}) copy-start(s32[128,2]{0,1:T(2,128)} %param.12) | copy-start | bytes 3076
  39.2 5.0 %copy-start.7 = (f32[16,8,2,16,128]{4,3,2,1,0:T(8,128)}, f32[16,8,2,16,128]{4,3,2,1,0:T(8,128)S(1)}, u32[]{:S(2)}) copy-start(f32[16,8,2,16,128]{4,3,2,1,0:T(8,128)S(1)} %all-to-all-done.2) | copy-start | bytes 6291460
  39.2 65.7 %all-to-all-start = ((f32[16,8,2,16,128]{4,3,2,1,0:T(8,128)}), f32[16,8,2,16,128]{4,3,2,1,0:T(8,128)}, u32[]{:S(2)}, u32[]{:S(2)}) async-start(f32[16,8,2,16,128]{4,3,2,1,0:T(8,128)} %cut_rows.2), calls=%async_computation | async-start | bytes 4194304 | tf_op jit(solution)/shard_map/all_to_all | solution.py:225
  44.5 2.1 copy-start.10
  56.2 41.9 %collective-permute-start.3 = (f32[54,1,2,16,128]{4,3,2,1,0:T(8,128)S(1)}, f32[54,1,2,16,128]{4,3,2,1,0:T(8,128)S(1)}, u32[]{:S(2)}, u32[]{:S(2)}) collective-permute-start(f32[54,1,2,16,128]{4,3,2,1,0:T(8,128)S(1)} %pick_leaving.4), channel_id=1, source_target_pairs={{0,16},{1,17},{2,18},{3,19},{4,20},{5,21},{6,22},{7,23},{8,24},{9,... | collective-permute-start | bytes 2654216 | tf_op jit(solution)/shard_map/ppermute | solution.py:228
  103.6 1.3 copy-start.3
  104.9 57.4 %all-to-all-start.3 = ((f32[16,8,1,2,16,128]{5,4,3,2,1,0:T(8,128)}), f32[16,8,1,2,16,128]{5,4,3,2,1,0:T(8,128)S(1)}, u32[]{:S(2)}, u32[]{:S(2)}) async-start(f32[16,8,1,2,16,128]{5,4,3,2,1,0:T(8,128)} %bitcast.12), calls=%async_computation.3 | async-start | bytes 4194304 | tf_op jit(solution)/shard_map/all_to_all | solution.py:221
  111.6 43.5 %collective-permute-start.2 = (f32[54,1,2,16,128]{4,3,2,1,0:T(8,128)}, f32[54,1,2,16,128]{4,3,2,1,0:T(8,128)}, u32[]{:S(2)}, u32[]{:S(2)}) collective-permute-start(f32[54,1,2,16,128]{4,3,2,1,0:T(8,128)} %pick_leaving.3), channel_id=1, source_target_pairs={{0,16},{1,17},{2,18},{3,19},{4,20},{5,21},{6,22},{7,23},{8,24},{9,... | collective-permute-start | bytes 2654216 | tf_op jit(solution)/shard_map/ppermute | solution.py:228
  160.9 1.4 copy-start.4
  162.3 49.5 %all-to-all-start.1 = ((f32[16,8,1,2,16,128]{5,4,3,2,1,0:T(8,128)}), f32[16,8,1,2,16,128]{5,4,3,2,1,0:T(8,128)}, u32[]{:S(2)}, u32[]{:S(2)}) async-start(f32[16,8,1,2,16,128]{5,4,3,2,1,0:T(8,128)} %bitcast.13), calls=%async_computation.1 | async-start | bytes 4194304 | tf_op jit(solution)/shard_map/all_to_all | solution.py:221
  170.7 35.5 %copy-start.8 = (f32[16,8,2,16,128]{4,3,2,1,0:T(8,128)S(1)}, f32[16,8,2,16,128]{4,3,2,1,0:T(8,128)}, u32[]{:S(2)}) copy-start(f32[16,8,2,16,128]{4,3,2,1,0:T(8,128)} %copy-done.7) | copy-start | bytes 6291460
  173.2 33.0 %collective-permute-start.4 = (f32[12,2,2,16,128]{4,3,2,1,0:T(8,128)S(1)}, f32[12,2,2,16,128]{4,3,2,1,0:T(8,128)S(1)}, u32[]{:S(2)}, u32[]{:S(2)}) collective-permute-start(f32[12,2,2,16,128]{4,3,2,1,0:T(8,128)S(1)} %pick_leaving.5), channel_id=1, source_target_pairs={{0,16},{1,17},{2,18},{3,19},{4,20},{5,21},{6,22},{7,23},{8,24},{9,... | collective-permute-start | bytes 1179656 | tf_op jit(solution)/shard_map/ppermute | solution.py:239
  210.5 1.3 copy-start.2
  211.8 4.7 %copy-start.12 = (s32[128]{0:T(128)S(1)}, s32[128]{0:T(128)}, u32[]{:S(2)}) copy-start(s32[128]{0:T(128)} %param.15) | copy-start | bytes 1540
  211.8 4.8 %copy-start.11 = (s32[128]{0:T(128)S(1)}, s32[128]{0:T(128)}, u32[]{:S(2)}) copy-start(s32[128]{0:T(128)} %param.14) | copy-start | bytes 1540
  211.8 33.8 %all-to-all-start.4 = ((f32[16,4,2,2,16,128]{5,4,3,2,1,0:T(8,128)}), f32[16,4,2,2,16,128]{5,4,3,2,1,0:T(8,128)}, u32[]{:S(2)}, u32[]{:S(2)}) async-start(f32[16,4,2,2,16,128]{5,4,3,2,1,0:T(8,128)} %bitcast.11), calls=%async_computation.4 | async-start | bytes 4194304 | tf_op jit(solution)/shard_map/all_to_all | solution.py:221
  216.9 2.2 copy-start.1
  231.0 1.4 copy-start.5
  245.6 1.6 copy-start.6

commit v5 on v4

--- a/solution.py
+++ b/solution.py
@@ -17,6 +17,7 @@
 SMEM = pl.BlockSpec(memory_space=pltpu.SMEM)
 VMEM = pl.BlockSpec(memory_space=pltpu.VMEM)
 PARAMS = pltpu.CompilerParams(vmem_limit_bytes=24 * 1024 * 1024)
+LARGE = pltpu.CompilerParams(vmem_limit_bytes=56 * 1024 * 1024)
 
 
 def cut_kernel(in_ref, out_ref):
@@ -139,52 +140,46 @@
     )(send, *spreads)
 
 
-def collect_kernel(parts, bounds, source_ref, *refs):
+def collect_kernel(parts, bounds, source_ref, crowded_ref, *refs):
     spread_refs, early_refs, extra_refs = (refs[i * parts : (i + 1) * parts] for i in range(3))
-    late_ref = refs[3 * parts] if bounds[2] > bounds[1] else None
+    here, early, late = bounds
+    late_ref = refs[3 * parts] if late > early else None
     out_ref, sem = refs[-2:]
-    here, early, late = bounds
 
     def copy(q, carry):
         source = source_ref[q]
-
-        @pl.when(source < here)
-        def _():
-            for c in range(parts):
-                out_ref[q, c] = spread_refs[c][source]
-
-        @pl.when((source >= here) & (source < early))
-        def _():
-            for c in range(parts):
-                out_ref[q, c] = early_refs[c][source - here, 0]
-
-        if late_ref is not None:
-
-            @pl.when((source >= early) & (source < late))
+        near = jnp.minimum(source, here - 1)
+        far = jnp.clip(source - here, 0, early - here - 1)
+        for c in range(parts):
+            value = jnp.where(source < here, spread_refs[c][near], early_refs[c][far, 0])
+            if late_ref is not None:
+                last = jnp.clip(source - early, 0, late - early - 1)
+                value = jnp.where(source < early, value, late_ref[last, c])
+            out_ref[q, c] = value
+        return carry
+
+    lax.fori_loop(0, out_ref.shape[0], copy, 0, unroll=4)
+
+    @pl.when(crowded_ref[0] > 0)
+    def _():
+        def fetch(q, carry):
+            source = source_ref[q] - late
+
+            @pl.when(source >= 0)
             def _():
                 for c in range(parts):
-                    out_ref[q, c] = late_ref[source - early, c]
-
-        return carry
-
-    lax.fori_loop(0, out_ref.shape[0], copy, 0)
-
-    def fetch(q, carry):
-        source = source_ref[q] - late
-
-        @pl.when(source >= 0)
-        def _():
-            for c in range(parts):
-                slow = pltpu.make_async_copy(extra_refs[c].at[source], out_ref.at[q, c], sem)
-                slow.start()
-                slow.wait()
-
-        return carry
-
-    lax.fori_loop(0, out_ref.shape[0], fetch, 0)
-
-
-def collect(source, spreads, earlies, extras, late, bounds):
+                    slow = pltpu.make_async_copy(
+                        extra_refs[c].at[source], out_ref.at[q, c], sem
+                    )
+                    slow.start()
+                    slow.wait()
+
+            return carry
+
+        lax.fori_loop(0, out_ref.shape[0], fetch, 0)
+
+
+def collect(source, crowded, spreads, earlies, extras, late, bounds):
     parts = len(spreads)
     arrays = [*spreads, *earlies, *extras]
     specs = [VMEM] * (2 * parts) + [ANY] * parts
@@ -193,7 +188,7 @@
         specs.append(VMEM)
     return pl.pallas_call(
         functools.partial(collect_kernel, parts, bounds),
-        in_specs=[SMEM] + specs,
+        in_specs=[SMEM, SMEM] + specs,
         out_specs=VMEM,
         out_shape=jax.ShapeDtypeStruct(
             (source.shape[0], parts) + spreads[0].shape[1:], jnp.float32
@@ -201,7 +196,7 @@
         scratch_shapes=[pltpu.SemaphoreType.DMA],
         compiler_params=PARAMS,
         name="collect",
-    )(source, *arrays)
+    )(source, crowded, *arrays)
 
 
 def fetch_items(cuts, early_ids, late_ids):
@@ -242,6 +237,7 @@
     for c in range(len(cuts)):
         picked = collect(
             early_source,
+            crowded,
             spreads[c : c + 1],
             earlies[c : c + 1],
             extras[c : c + 1],
@@ -249,7 +245,7 @@
             (count, count + rooms[0], count + rooms[0]),
         )
         delivered.append(exchange(picked))
-    picked = collect(late_source, spreads, earlies, extras, late, bounds)
+    picked = collect(late_source, crowded, spreads, earlies, extras, late, bounds)
     last = exchange(picked)
     return delivered, last
 
@@ -352,7 +348,7 @@
             out_specs=pl.BlockSpec(whole, lambda k, t, s: (0, 0, 0, 0)),
         ),
         out_shape=jax.ShapeDtypeStruct(whole, jnp.float32),
-        compiler_params=PARAMS,
+        compiler_params=LARGE,
         name="finish",
     )(target, sign, lefts, right)
 

time: 255 us -> 248 us (0.973)
  Pallas kernels: 55.3 us -> 49.5 us
    pallas_call x3, Pallas kernels: 15.5 us -> 9.3 us  [collect(): pl.pallas_call(functools.partial(collect_kernel, parts, bounds), in_specs...]
    unnamed x26 -> x24, local copies, waits for them, and re-layouts: 9.18 us -> 7.63 us
  transfers between devices with their start and end apart: 8 -> 8, of which waited for: 5 -> 5; matrix products, arithmetic and copies ran while one was open for 3% -> 3% of each run, Pallas kernels for 18% -> 16%
where the time goes in v5:
time: 248 us; the launch traced here: 247 us
  waiting for transfers between devices  146 us (59%)
  Pallas kernels  49.5 us (20%)
  starting transfers between devices  34.5 us (14%)
  local copies, waits for them, and re-layouts  15.2 us (6%)
    ppermute x2, waiting for transfers between devices, fetch_items(): earlies.append(lax.ppermute(leaving, 'node', swap))  75.5 us
    ppermute x1, waiting for transfers between devices, fetch_items(): late = lax.ppermute(leaving, 'node', swap)  32.9 us
    all_to_all x2, waiting for transfers between devices, fetch_items(): lax.all_to_all(cut, 'node', 0, 0, axis_index_groups=halves, tiled=True)  25.2 us
    all_to_all x3, starting transfers between devices, exchange(): return lax.all_to_all(x, 'node', 0, 0, axis_index_groups=halves, tiled=True)  17.1 us
    all_to_all x3, waiting for transfers between devices, exchange(): return lax.all_to_all(x, 'node', 0, 0, axis_index_groups=halves, tiled=True)  12.2 us
    pallas_call x2, Pallas kernels, multiply(): pl.pallas_call(multiply_kernel, grid_spec=pltpu.PrefetchScalarGridSpec(nu...  11.9 us
    all_to_all x2, starting transfers between devices, fetch_items(): lax.all_to_all(cut, 'node', 0, 0, axis_index_groups=halves, tiled=True)  11.3 us
    pallas_call x3, Pallas kernels, collect(): pl.pallas_call(functools.partial(collect_kernel, parts, bounds), in_specs...  9.3 us
  transfers between devices with their start and end apart: 8, of which 5 were waited for; matrix products, arithmetic and copies ran while one was open for 3% of the time, Pallas kernels for 16%

profile of v5, /device:TPU:0, one launch (start us, length us, event | category | flops | bytes accessed | tf_op | source)
XLA Modules:
  0.0 246.8 jit_solution(8884777051652422110)
XLA Ops:
  0.0 3.9 %cut_rows.3 = f32[16,8,2,16,128]{4,3,2,1,0:T(8,128)} custom-call(f32[8,2,256,256]{3,2,1,0:T(8,128)} %left_ref.1), custom_call_target="tpu_custom_call" | custom-call | tf_op jit(solution)/shard_map/cut_rows/pallas_call | solution.py:33
  3.9 6.3 %all-to-all-start.2 = ((f32[16,8,2,16,128]{4,3,2,1,0:T(8,128)}), f32[16,8,2,16,128]{4,3,2,1,0:T(8,128)S(1)}, u32[]{:S(2)}, u32[]{:S(2)}) async-start(f32[16,8,2,16,128]{4,3,2,1,0:T(8,128)} %cut_rows.3), calls=%async_computation.2 | async-start | bytes 4194304 | tf_op jit(solution)/shard_map/all_to_all | solution.py:220
  10.2 3.8 %cut_rows.2 = f32[16,8,2,16,128]{4,3,2,1,0:T(8,128)} custom-call(f32[8,2,256,256]{3,2,1,0:T(8,128)} %left_ref.1), custom_call_target="tpu_custom_call" | custom-call | tf_op jit(solution)/shard_map/cut_rows/pallas_call | solution.py:33
  14.0 25.2 %all-to-all-done.2 = f32[16,8,2,16,128]{4,3,2,1,0:T(8,128)S(1)} async-done(((f32[16,8,2,16,128]{4,3,2,1,0:T(8,128)}), f32[16,8,2,16,128]{4,3,2,1,0:T(8,128)S(1)}, u32[]{:S(2)}, u32[]{:S(2)}) %all-to-all-start.2) | async-done | bytes 2097184 | tf_op jit(solution)/shard_map/all_to_all | solution.py:220
  39.3 5.0 %all-to-all-start = ((f32[16,8,2,16,128]{4,3,2,1,0:T(8,128)}), f32[16,8,2,16,128]{4,3,2,1,0:T(8,128)}, u32[]{:S(2)}, u32[]{:S(2)}) async-start(f32[16,8,2,16,128]{4,3,2,1,0:T(8,128)} %cut_rows.2), calls=%async_computation | async-start | bytes 4194304 | tf_op jit(solution)/shard_map/all_to_all | solution.py:220
  44.5 1.9 gather_fusion
  48.1 6.4 %make_plan.1 = (s32[128]{0:T(128)S(1)}, s32[128]{0:T(128)S(1)}, s32[128]{0:T(128)S(1)}, s32[64]{0:T(128)S(1)}, s32[1]{0:T(128)}) custom-call(s32[1]{0:T(128)} %bitcast.1.half_ref, s32[256]{0:T(256)S(1)} %reshape.36.refs_0_, s32[128]{0:T(128)S(1)} %get-tuple-element.23.refs_1_), custom_call_target="tpu_custom_call" | custom-call | tf_op jit(solution)/shard_map/make_plan/pallas_call | solution.py:104
  54.5 1.7 pick_leaving.4
  56.3 2.7 %collective-permute-start.3 = (f32[54,1,2,16,128]{4,3,2,1,0:T(8,128)S(1)}, f32[54,1,2,16,128]{4,3,2,1,0:T(8,128)S(1)}, u32[]{:S(2)}, u32[]{:S(2)}) collective-permute-start(f32[54,1,2,16,128]{4,3,2,1,0:T(8,128)S(1)} %pick_leaving.4), channel_id=1, source_target_pairs={{0,16},{1,17},{2,18},{3,19},{4,20},{5,21},{6,22},{7,23},{8,24},{9,... | collective-permute-start | bytes 2654216 | tf_op jit(solution)/shard_map/ppermute | solution.py:223
  59.6 1.6 conditional.3
  59.6 1.6 broadcast.12
  61.2 36.9 %collective-permute-done.3.refs_1_.refs_3_ = f32[54,1,2,16,128]{4,3,2,1,0:T(8,128)S(1)} collective-permute-done((f32[54,1,2,16,128]{4,3,2,1,0:T(8,128)S(1)}, f32[54,1,2,16,128]{4,3,2,1,0:T(8,128)S(1)}, u32[]{:S(2)}, u32[]{:S(2)}) %collective-permute-start.3) | collective-permute-done | bytes 884768 | tf_op jit(solution)/shard_map/ppermute | solution.py:223
  98.1 3.0 %collect.4 = f32[128,1,2,16,128]{4,3,2,1,0:T(8,128)S(1)} custom-call(s32[128]{0:T(128)S(1)} %get-tuple-element.18.source_ref, s32[1]{0:T(128)} %get-tuple-element.19.crowded_ref, f32[128,2,16,128]{3,2,1,0:T(8,128)} %bitcast.16, f32[54,1,2,16,128]{4,3,2,1,0:T(8,128)S(1)} %collective-permute-done.3.refs_1_.refs_3_, ...), custom_call_target="tpu_custom_call" | custom-call | tf_op jit(solution)/shard_map/collect/pallas_call | solution.py:189
  101.2 1.4 copy-done.3
  102.6 4.0 %all-to-all-start.3 = ((f32[16,8,1,2,16,128]{5,4,3,2,1,0:T(8,128)}), f32[16,8,1,2,16,128]{5,4,3,2,1,0:T(8,128)S(1)}, u32[]{:S(2)}, u32[]{:S(2)}) async-start(f32[16,8,1,2,16,128]{5,4,3,2,1,0:T(8,128)} %bitcast.12), calls=%async_computation.3 | async-start | bytes 4194304 | tf_op jit(solution)/shard_map/all_to_all | solution.py:216
  106.6 2.7 %pick_leaving.3 = f32[54,1,2,16,128]{4,3,2,1,0:T(8,128)} custom-call(s32[128]{0:T(128)S(1)} %get-tuple-element.20.send_ref, f32[128,2,16,128]{3,2,1,0:T(8,128)} %bitcast.3.refs_0_), custom_call_target="tpu_custom_call" | custom-call | tf_op jit(solution)/shard_map/pick_leaving/pallas_call | solution.py:133
  109.2 3.4 %collective-permute-start.2 = (f32[54,1,2,16,128]{4,3,2,1,0:T(8,128)}, f32[54,1,2,16,128]{4,3,2,1,0:T(8,128)}, u32[]{:S(2)}, u32[]{:S(2)}) collective-permute-start(f32[54,1,2,16,128]{4,3,2,1,0:T(8,128)} %pick_leaving.3), channel_id=1, source_target_pairs={{0,16},{1,17},{2,18},{3,19},{4,20},{5,21},{6,22},{7,23},{8,24},{9,... | collective-permute-start | bytes 2654216 | tf_op jit(solution)/shard_map/ppermute | solution.py:223
  112.6 1.6 conditional.2
  112.6 1.6 broadcast.11
  114.2 38.5 %collective-permute-done.2.refs_1_.refs_2_ = f32[54,1,2,16,128]{4,3,2,1,0:T(8,128)} collective-permute-done((f32[54,1,2,16,128]{4,3,2,1,0:T(8,128)}, f32[54,1,2,16,128]{4,3,2,1,0:T(8,128)}, u32[]{:S(2)}, u32[]{:S(2)}) %collective-permute-start.2) | collective-permute-done | bytes 884768 | tf_op jit(solution)/shard_map/ppermute | solution.py:223
  152.7 3.2 %collect.3 = f32[128,1,2,16,128]{4,3,2,1,0:T(8,128)S(1)} custom-call(s32[128]{0:T(128)S(1)} %get-tuple-element.18.source_ref, s32[1]{0:T(128)} %get-tuple-element.19.crowded_ref, f32[128,2,16,128]{3,2,1,0:T(8,128)} %bitcast.3.refs_0_, f32[54,1,2,16,128]{4,3,2,1,0:T(8,128)} %collective-permute-done.2.refs_1_.refs_2_, ...), custom_call_target="tpu_custom_call" | custom-call | tf_op jit(solution)/shard_map/collect/pallas_call | solution.py:189
  157.3 8.4 %all-to-all-start.1 = ((f32[16,8,1,2,16,128]{5,4,3,2,1,0:T(8,128)}), f32[16,8,1,2,16,128]{5,4,3,2,1,0:T(8,128)}, u32[]{:S(2)}, u32[]{:S(2)}) async-start(f32[16,8,1,2,16,128]{5,4,3,2,1,0:T(8,128)} %bitcast.13), calls=%async_computation.1 | async-start | bytes 4194304 | tf_op jit(solution)/shard_map/all_to_all | solution.py:216
  165.8 2.4 pick_leaving.5
  168.3 32.9 %collective-permute-done.4.refs_6_ = f32[12,2,2,16,128]{4,3,2,1,0:T(8,128)S(1)} collective-permute-done((f32[12,2,2,16,128]{4,3,2,1,0:T(8,128)S(1)}, f32[12,2,2,16,128]{4,3,2,1,0:T(8,128)S(1)}, u32[]{:S(2)}, u32[]{:S(2)}) %collective-permute-start.4) | collective-permute-done | bytes 393248 | tf_op jit(solution)/shard_map/ppermute | solution.py:234
  201.2 3.1 %collect.5 = f32[64,2,2,16,128]{4,3,2,1,0:T(8,128)S(1)} custom-call(s32[64]{0:T(128)S(1)} %get-tuple-element.21.source_ref, s32[1]{0:T(128)} %get-tuple-element.19.crowded_ref, f32[128,2,16,128]{3,2,1,0:T(8,128)} %bitcast.3.refs_0_, f32[128,2,16,128]{3,2,1,0:T(8,128)S(1)} %bitcast.18, f32[54,1,2,16,128]{4,3,2,1,0:T(8,128)} %collective-permute-done.2.refs_1_.refs_2_, ...), custom_call_target="tpu_custom_call" | custom-call | tf_op jit(solution)/shard_map/collect/pallas_call | solution.py:189
  205.6 4.7 %all-to-all-start.4 = ((f32[16,4,2,2,16,128]{5,4,3,2,1,0:T(8,128)}), f32[16,4,2,2,16,128]{5,4,3,2,1,0:T(8,128)}, u32[]{:S(2)}, u32[]{:S(2)}) async-start(f32[16,4,2,2,16,128]{5,4,3,2,1,0:T(8,128)} %bitcast.11), calls=%async_computation.4 | async-start | bytes 4194304 | tf_op jit(solution)/shard_map/all_to_all | solution.py:216
  211.8 2.2 copy-done.1
  214.0 6.0 %multiply.2.left_ref = f32[4,2,256,256]{3,2,1,0:T(8,128)S(1)} custom-call(s32[4]{0:T(128)S(1)} %subtract_reduce_fusion.first_ref, f32[8,2,256,256]{3,2,1,0:T(8,128)S(1)} %copy-done.1, f32[16,8,1,2,16,128]{5,4,3,2,1,0:T(8,128)} %all-to-all-done.1.refs_0_, f32[16,8,1,2,16,128]{5,4,3,2,1,0:T(8,128)S(1)} %all-to-all-done.3.refs_1_), custom_call_target="tpu_custom_call" | custom-call | tf_op jit(solution)/shard_map/multiply/pallas_call | solution.py:302
  219.9 6.0 %multiply.3.left_ref = f32[4,2,256,256]{3,2,1,0:T(8,128)S(1)} custom-call(s32[4]{0:T(128)S(1)} %subtract_bitcast_fusion.first_ref, f32[4,2,256,256]{3,2,1,0:T(8,128)S(1)} %multiply.2.left_ref, f32[16,8,1,2,16,128]{5,4,3,2,1,0:T(8,128)} %all-to-all-done.1.refs_0_, f32[16,8,1,2,16,128]{5,4,3,2,1,0:T(8,128)S(1)} %all-to-all-done.3.refs_1_), custom_call_target="tpu_custom_call" | custom-call | tf_op jit(solution)/shard_map/multiply/pallas_call | solution.py:302
  225.9 1.3 copy-done.5
  227.3 12.2 %all-to-all-done.4.right_ref = f32[16,4,2,2,16,128]{5,4,3,2,1,0:T(8,128)} async-done(((f32[16,4,2,2,16,128]{5,4,3,2,1,0:T(8,128)}), f32[16,4,2,2,16,128]{5,4,3,2,1,0:T(8,128)}, u32[]{:S(2)}, u32[]{:S(2)}) %all-to-all-start.4) | async-done | bytes 2097184 | tf_op jit(solution)/shard_map/all_to_all | solution.py:216
  239.5 7.3 %finish.1 = f32[2,2,256,256]{3,2,1,0:T(8,128)} custom-call(s32[4]{0:T(128)} %dynamic-slice_subtract_fusion.target, s32[4]{0:T(128)} %dynamic_slice.13.sign, f32[4,2,256,256]{3,2,1,0:T(8,128)} %copy-done.5, f32[16,4,2,2,16,128]{5,4,3,2,1,0:T(8,128)} %all-to-all-done.4.right_ref), custom_call_target="tpu_custom_call" | custom-call | tf_op jit(solution)/shard_map/finish/pallas_call | solution.py:339
  (45 shorter events, 6.0 us)
Async XLA Ops:
  0.0 44.5 %copy-start = (s32[256]{0:T(256)S(1)}, s32[256]{0:T(256)}, u32[]{:S(2)}) copy-start(s32[256]{0:T(256)} %param.11) | copy-start | bytes 3076
  3.9 35.4 %all-to-all-start.2 = ((f32[16,8,2,16,128]{4,3,2,1,0:T(8,128)}), f32[16,8,2,16,128]{4,3,2,1,0:T(8,128)S(1)}, u32[]{:S(2)}, u32[]{:S(2)}) async-start(f32[16,8,2,16,128]{4,3,2,1,0:T(8,128)} %cut_rows.3), calls=%async_computation.2 | async-start | bytes 4194304 | tf_op jit(solution)/shard_map/all_to_all | solution.py:220
  14.0 30.2 %copy-start.8 = (s32[128,2]{0,1:T(2,128)S(1)}, s32[128,2]{0,1:T(2,128)}, u32[]{:S(2)}) copy-start(s32[128,2]{0,1:T(2,128)} %param.12) | copy-start | bytes 3076
  39.2 5.0 %copy-start.6 = (f32[16,8,2,16,128]{4,3,2,1,0:T(8,128)}, f32[16,8,2,16,128]{4,3,2,1,0:T(8,128)S(1)}, u32[]{:S(2)}) copy-start(f32[16,8,2,16,128]{4,3,2,1,0:T(8,128)S(1)} %all-to-all-done.2) | copy-start | bytes 6291460
  39.3 63.3 %all-to-all-start = ((f32[16,8,2,16,128]{4,3,2,1,0:T(8,128)}), f32[16,8,2,16,128]{4,3,2,1,0:T(8,128)}, u32[]{:S(2)}, u32[]{:S(2)}) async-start(f32[16,8,2,16,128]{4,3,2,1,0:T(8,128)} %cut_rows.2), calls=%async_computation | async-start | bytes 4194304 | tf_op jit(solution)/shard_map/all_to_all | solution.py:220
  44.5 2.1 copy-start.9
  56.3 41.9 %collective-permute-start.3 = (f32[54,1,2,16,128]{4,3,2,1,0:T(8,128)S(1)}, f32[54,1,2,16,128]{4,3,2,1,0:T(8,128)S(1)}, u32[]{:S(2)}, u32[]{:S(2)}) collective-permute-start(f32[54,1,2,16,128]{4,3,2,1,0:T(8,128)S(1)} %pick_leaving.4), channel_id=1, source_target_pairs={{0,16},{1,17},{2,18},{3,19},{4,20},{5,21},{6,22},{7,23},{8,24},{9,... | collective-permute-start | bytes 2654216 | tf_op jit(solution)/shard_map/ppermute | solution.py:223
  101.2 1.4 copy-start.3
  102.6 54.8 %all-to-all-start.3 = ((f32[16,8,1,2,16,128]{5,4,3,2,1,0:T(8,128)}), f32[16,8,1,2,16,128]{5,4,3,2,1,0:T(8,128)S(1)}, u32[]{:S(2)}, u32[]{:S(2)}) async-start(f32[16,8,1,2,16,128]{5,4,3,2,1,0:T(8,128)} %bitcast.12), calls=%async_computation.3 | async-start | bytes 4194304 | tf_op jit(solution)/shard_map/all_to_all | solution.py:216
  109.2 43.5 %collective-permute-start.2 = (f32[54,1,2,16,128]{4,3,2,1,0:T(8,128)}, f32[54,1,2,16,128]{4,3,2,1,0:T(8,128)}, u32[]{:S(2)}, u32[]{:S(2)}) collective-permute-start(f32[54,1,2,16,128]{4,3,2,1,0:T(8,128)} %pick_leaving.3), channel_id=1, source_target_pairs={{0,16},{1,17},{2,18},{3,19},{4,20},{5,21},{6,22},{7,23},{8,24},{9,... | collective-permute-start | bytes 2654216 | tf_op jit(solution)/shard_map/ppermute | solution.py:223
  156.0 1.4 copy-start.4
  157.3 48.3 %all-to-all-start.1 = ((f32[16,8,1,2,16,128]{5,4,3,2,1,0:T(8,128)}), f32[16,8,1,2,16,128]{5,4,3,2,1,0:T(8,128)}, u32[]{:S(2)}, u32[]{:S(2)}) async-start(f32[16,8,1,2,16,128]{5,4,3,2,1,0:T(8,128)} %bitcast.13), calls=%async_computation.1 | async-start | bytes 4194304 | tf_op jit(solution)/shard_map/all_to_all | solution.py:216
  165.8 35.5 %copy-start.7 = (f32[16,8,2,16,128]{4,3,2,1,0:T(8,128)S(1)}, f32[16,8,2,16,128]{4,3,2,1,0:T(8,128)}, u32[]{:S(2)}) copy-start(f32[16,8,2,16,128]{4,3,2,1,0:T(8,128)} %copy-done.6) | copy-start | bytes 6291460
  168.2 33.0 %collective-permute-start.4 = (f32[12,2,2,16,128]{4,3,2,1,0:T(8,128)S(1)}, f32[12,2,2,16,128]{4,3,2,1,0:T(8,128)S(1)}, u32[]{:S(2)}, u32[]{:S(2)}) collective-permute-start(f32[12,2,2,16,128]{4,3,2,1,0:T(8,128)S(1)} %pick_leaving.5), channel_id=1, source_target_pairs={{0,16},{1,17},{2,18},{3,19},{4,20},{5,21},{6,22},{7,23},{8,24},{9,... | collective-permute-start | bytes 1179656 | tf_op jit(solution)/shard_map/ppermute | solution.py:234
  204.3 1.3 copy-start.2
  205.6 4.7 %copy-start.11 = (s32[128]{0:T(128)S(1)}, s32[128]{0:T(128)}, u32[]{:S(2)}) copy-start(s32[128]{0:T(128)} %param.15) | copy-start | bytes 1540
  205.6 5.4 %copy-start.10 = (s32[128]{0:T(128)S(1)}, s32[128]{0:T(128)}, u32[]{:S(2)}) copy-start(s32[128]{0:T(128)} %param.14) | copy-start | bytes 1540
  205.6 33.8 %all-to-all-start.4 = ((f32[16,4,2,2,16,128]{5,4,3,2,1,0:T(8,128)}), f32[16,4,2,2,16,128]{5,4,3,2,1,0:T(8,128)}, u32[]{:S(2)}, u32[]{:S(2)}) async-start(f32[16,4,2,2,16,128]{5,4,3,2,1,0:T(8,128)} %bitcast.11), calls=%async_computation.4 | async-start | bytes 4194304 | tf_op jit(solution)/shard_map/all_to_all | solution.py:216
  211.8 2.2 copy-start.1
  225.9 1.4 copy-start.5
